TPU v7x, 32 devices: a whole 2x2x4 slice. The times are simulated.
32 devices in a mesh: rep: 4 (over z), row: 4 (over y, core), col: 2 (over x).
Axes of the slice: x: 2, y: 2, z: 4, core: 2. Of those that a mesh axis runs over, the one named last changes fastest.
Arguments:
- weights: bfloat16 [4, 4096, 2048], P('rep', 'row', 'col'), may hold values from -3 to 3
- tracker: bfloat16 [4, 4096, 2048], P('rep', 'row', 'col'), may hold values from -6 to 6
- grad_prev: bfloat16 [4, 4096, 2048], P('rep', 'row', 'col'), may hold values from -6 to 6
- pool: bfloat16 [4, 1024, 2048], P('rep', 'row', 'col'), may hold values from -6 to 6
- out_grads: bfloat16 [4, 2, 512, 4096], P('rep', None, 'col', 'row'), may hold values from -0.25 to 0.25
- row_ids: int32 [4, 2, 512], P('rep'), may hold values from 0 to 1023
- step_index: int32 [1], replicated, may hold values from 0 to 999
Outputs:
- new_weights: bfloat16 [4, 4096, 2048], P('rep', 'row', 'col')
- new_tracker: bfloat16 [4, 4096, 2048], P('rep', 'row', 'col')
Inputs may be any that keep to these rules, and one draw needn't show every extreme that they name: `row_ids`: rows may repeat and need not all be used.
All inputs are finite; a program needn't handle non-finite values.
Results may differ from a plain program's by a relative error of at most 0.0085.
Values may be sent and summed in bfloat16 or wider, within the bound.
No kernel may reach another device: no remote copies, remote signals or barrier semaphores. Data moves between devices by JAX's collectives and lax.ppermute only.
A program may use at most 128 MiB of HBM per device.

v0:
```python
import functools
import math

import jax
import jax.numpy as jnp
from jax import lax
from jax.sharding import PartitionSpec as P

D = 2048
QOUT = 4096
GRID = 4
NS_ITERS = 2
STEPS = 2


quintic_a = 3.4445
quintic_b = -4.775
quintic_c = 2.0315


def for_sending(x):
    return jax.tree.map(lambda a: a.astype(jnp.bfloat16) if a.dtype == jnp.float32 else a, x)


def partner(block, axis, distance):
    count = lax.axis_size(axis)
    route = []
    for low in range(count):
        high = low | 1 << distance
        if high != low and high < count:
            route += [(low, high), (high, low)]
    return lax.ppermute(block, axis, route)


def orthogonalize(mixed):
    shard_rows, shard_cols = mixed.shape
    block_rows = QOUT // GRID
    block_cols = D // GRID
    blocks = mixed.astype(jnp.float32).reshape(
        shard_rows // block_rows, block_rows, shard_cols // block_cols, block_cols
    )
    norm = jnp.sqrt(jnp.sum(blocks * blocks, axis=(1, 3), keepdims=True)) + 1e-07
    iterate = (blocks / norm).astype(jnp.bfloat16)
    for turn in range(NS_ITERS):
        gram = jnp.einsum(
            "rizc,rizd->rzcd", iterate, iterate, preferred_element_type=jnp.float32
        ).astype(jnp.bfloat16)
        square = jnp.einsum("rzcd,rzde->rzce", gram, gram, preferred_element_type=jnp.float32)
        poly = (quintic_b * gram.astype(jnp.float32) + quintic_c * square).astype(jnp.bfloat16)
        product = jnp.einsum("rizc,rzcd->rizd", iterate, poly, preferred_element_type=jnp.float32)
        iterate = (quintic_a * iterate.astype(jnp.float32) + product).astype(jnp.bfloat16)
    return iterate.reshape(shard_rows, shard_cols)


def gradient_at(pool_all, out_grad, chosen_ids):
    chosen = jnp.take(pool_all, chosen_ids, axis=0)
    return lax.dot_general(
        lax.all_gather(out_grad, "col", axis=0, tiled=True),
        chosen,
        (((0,), (0,)), ((), ())),
        preferred_element_type=jnp.float32,
    )


def swap_states(value, level):
    return partner((for_sending(value[0]), for_sending(value[1])), "rep", level)


def partner_value(helper, value, bit, levels):
    branches = [functools.partial(helper, level=level) for level in range(levels)]
    return lax.switch(bit, branches, value)


def body(weights, tracker, grad_prev, pool, out_grads, row_ids, step_index):
    own_weights = weights[0]
    own_tracker = tracker[0]
    pool_all = lax.all_gather(pool[0], "row", axis=0, tiled=True)
    levels = lax.axis_size("rep").bit_length() - 1
    scale = 0.2 * math.sqrt(QOUT // GRID)
    older = grad_prev[0].astype(jnp.float32)
    for step in range(STEPS):
        bit = (step_index[0] + step) % levels
        fresh = gradient_at(pool_all, out_grads[0, step], row_ids[0, step])
        other_weights, other_tracker = partner_value(
            swap_states, (own_weights, own_tracker), bit, levels
        )
        mixed = (
            0.5 * (own_tracker.astype(jnp.float32) + other_tracker.astype(jnp.float32))
            + fresh
            - older
        ).astype(jnp.bfloat16)
        update = orthogonalize(mixed)
        moved = 0.5 * (
            own_weights.astype(jnp.float32) + other_weights.astype(jnp.float32)
        ) - scale * update.astype(jnp.float32)
        own_weights = moved.astype(jnp.bfloat16)
        own_tracker = mixed
        older = fresh
    return (own_weights[None], own_tracker[None])


def solution(mesh):
    in_specs = (
        P("rep", "row", "col"),
        P("rep", "row", "col"),
        P("rep", "row", "col"),
        P("rep", "row", "col"),
        P("rep", None, "col", "row"),
        P("rep", None, None),
        P(),
    )
    out_specs = (P("rep", "row", "col"), P("rep", "row", "col"))
    return jax.shard_map(body, mesh=mesh, in_specs=in_specs, out_specs=out_specs, check_vma=False)
```

profile of v0, /device:TPU:0, one launch (start us, length us, event | category | flops | bytes accessed | tf_op | source)
XLA Modules:
  0.0 414.3 jit_solution(12830962260510539033)
XLA Ops:
  7.2 0.0 copy-start.8
  7.2 0.0 copy-start.7
  7.2 0.0 all-gather.7.cloned.1.call-start
  7.2 0.7 all-gather.7.cloned.1.call-update
  7.9 0.0 all-gather.9.cloned.1.call-start
  8.0 2.3 fusion.45
  10.3 0.0 all-gather.9.cloned.1.call-update
  10.3 0.0 all-gather.11.cloned.1.call-start
  10.3 0.7 all-gather.11.cloned.1.call-update
  11.7 0.0 copy-done.8
  11.8 0.0 copy-done.7
  11.8 2.6 copy.46
  14.3 2.9 copy.38
  17.2 0.0 copy-start.1
  17.2 4.7 %copy.39 = bf16[1,1024,1024]{1,2,0:T(8,128)(2,1)} copy(bf16[1,1024,1024]{2,1,0:T(8,128)(2,1)} %param.14) | data formatting | bytes 4194304 | tf_op args[1]
  21.9 0.0 copy-done.1
  21.9 190.4 %conditional.6 = (f32[1024,1024]{0,1:T(8,128)}, f32[1024,1024]{0,1:T(8,128)}) conditional(s32[]{:T(128)} %clamp.6, (bf16[1024,1024]{0,1:T(8,128)(2,1)S(1)}, bf16[1024,1024]{0,1:T(8,128)(2,1)}) %tuple.99, (bf16[1024,1024]{0,1:T(8,128)(2,1)S(1)}, bf16[1024,1024]{0,1:T(8,128)(2,1)}) %tuple.100), branch_computations={%region_0.1_spmd, %region_1.2_spmd} | conditional | bytes 37748832
  22.0 2.6 copy.42
  24.5 4.0 collective-permute-start.2
  28.5 4.0 copy.43
  32.5 0.0 collective-permute-start.3
  32.5 132.7 %collective-permute-done.2 = bf16[1024,1024]{1,0:T(8,128)(2,1)} collective-permute-done((bf16[1024,1024]{1,0:T(8,128)(2,1)}, bf16[1024,1024]{1,0:T(8,128)(2,1)}, u32[]{:S(2)}, u32[]{:S(2)}) %collective-permute-start.2) | collective-permute-done | bytes 2097184 | tf_op jit(solution)/shard_map/cond/branch_1_fun/ppermute | solution.py:32
  165.2 4.2 %copy.78 = f32[1024,1024]{0,1:T(8,128)} copy(bf16[1024,1024]{1,0:T(8,128)(2,1)} %collective-permute-done.2) | data formatting | bytes 6291456 | tf_op jit(solution)/shard_map/conditional.2
  169.4 39.9 %collective-permute-done.3 = bf16[1024,1024]{1,0:T(8,128)(2,1)S(1)} collective-permute-done((bf16[1024,1024]{1,0:T(8,128)(2,1)}, bf16[1024,1024]{1,0:T(8,128)(2,1)S(1)}, u32[]{:S(2)}, u32[]{:S(2)}) %collective-permute-start.3) | collective-permute-done | bytes 2097184 | tf_op jit(solution)/shard_map/cond/branch_1_fun/ppermute | solution.py:32
  209.3 3.1 copy.80
  212.3 4.7 %gather_fusion = bf16[512,1024]{1,0:T(8,128)(2,1)S(1)} fusion(bf16[1024,1024]{1,0:T(8,128)(2,1)} %bitcast.113, s32[1024]{0:T(1024)S(1)} %pad_clamp_fusion.1), kind=kCustom, calls=%fused_computation.clone | custom fusion | bytes 2099200 | tf_op jit(solution)/shard_map/jit(_take)/gather | solution.py:56
  217.1 0.0 copy-done
  217.1 2.8 gather_fusion.1
  219.8 7.7 %multiply_reduce_fusion.1 = (f32[1024]{0:T(1024)S(1)}, bf16[1024,1024]{0,1:T(8,128)(2,1)S(1)}, f32[1024,1024]{1,0:T(8,128)}) fusion(bf16[1,1024,1024]{1,2,0:T(8,128)(2,1)} %copy.46, f32[1024,1024]{0,1:T(8,128)} %get-tuple-element.84, bf16[1,1024,1024]{1,2,0:T(8,128)(2,1)} %copy.39, bf16[1,1,512,1024]{3,2,1,0:T(8,128)(2,1)} %all-gather.9.cloned.1.call-done, ...), kind=kOutput, calls=%fused_computation.27 | convolution fusion | flops 1084750848 | bytes 16781824 | tf_op jit(solution)/shard_map/dot_general | solution.py:57
  227.5 2.4 convert_element_type.207
  230.0 5.4 %copy.47 = f32[1024,2,512]{2,0,1:T(8,128)} copy(f32[1024,2,512]{0,2,1:T(8,128)} %bitcast.120) | data formatting | bytes 8388608 | tf_op jit(solution)/shard_map/reshape | solution.py:39
  235.4 0.1 reduce_sum.25
  235.5 2.8 divide_convert_fusion.2
  238.3 0.0 copy-start.6
  238.3 1.3 convolution_convert_fusion.1
  239.6 0.0 copy-done.6
  239.6 5.6 %fusion.3 = bf16[1,1024,2,512]{1,3,2,0:T(8,128)(2,1)} fusion(bf16[1024,2,512]{2,0,1:T(8,128)(2,1)} %copy-done.6, f32[1,1024,2,512]{1,3,2,0:T(8,128)} %bitcast.121, f32[2]{0:T(128)S(1)} %sqrt_add_fusion.1, bf16[2,512,512]{2,1,0:T(8,128)(2,1)S(1)} %convolution_convert_fusion.1), kind=kOutput, calls=%fused_computation.9 | convolution fusion | flops 1619525632 | bytes 9437192 | tf_op jit(solution)/shard_map/rizc,rzcd->rizd/dot_general | solution.py:50
  245.3 3.5 fusion.19
  248.8 6.2 %convert_multiply_fusion.1 = f32[1,1024,2,512]{1,3,2,0:T(8,128)} fusion(bf16[1,1024,2,512]{1,3,2,0:T(8,128)(2,1)} %fusion.3, bf16[2,512,512]{2,1,0:T(8,128)(2,1)S(1)} %fusion.19), kind=kOutput, calls=%fused_computation.24 | convolution fusion | flops 1619525632 | bytes 7340032 | tf_op jit(solution)/shard_map/rizc,rzcd->rizd/dot_general | solution.py:50
  255.0 6.6 %fusion.8 = bf16[1024,1024]{0,1:T(8,128)(2,1)} fusion(f32[1,1024,2,512]{1,3,2,0:T(8,128)} %convert_multiply_fusion.1, f32[1024,1024]{0,1:T(8,128)} %get-tuple-element.83, bf16[1,1024,1024]{1,2,0:T(8,128)(2,1)} %copy-done.1), kind=kLoop, calls=%fused_computation.18 | loop fusion | flops 5242880 | bytes 12582912 | tf_op jit(solution)/shard_map/convert_element_type | solution.py:96
  261.6 100.3 %conditional.7 = (f32[1024,1024]{0,1:T(8,128)}, f32[1024,1024]{0,1:T(8,128)}) conditional(s32[]{:T(128)} %clamp.7, (bf16[1024,1024]{0,1:T(8,128)(2,1)}, bf16[1024,1024]{0,1:T(8,128)(2,1)S(1)}) %tuple.54, (bf16[1024,1024]{0,1:T(8,128)(2,1)}, bf16[1024,1024]{0,1:T(8,128)(2,1)S(1)}) %tuple.54), branch_computations={%region_4.6_spmd, %region_5.7_spmd} | conditional | bytes 37748832
  261.6 4.0 copy.53
  265.7 0.8 collective-permute-start.4
  266.5 2.6 copy.54
  269.1 1.2 collective-permute-start.5
  270.3 44.2 %collective-permute-done.4 = bf16[1024,1024]{1,0:T(8,128)(2,1)} collective-permute-done((bf16[1024,1024]{1,0:T(8,128)(2,1)}, bf16[1024,1024]{1,0:T(8,128)(2,1)}, u32[]{:S(2)}, u32[]{:S(2)}) %collective-permute-start.4) | collective-permute-done | bytes 2097184 | tf_op jit(solution)/shard_map/cond/branch_0_fun/ppermute | solution.py:32
  314.5 4.1 copy.81
  318.6 39.2 %collective-permute-done.5 = bf16[1024,1024]{1,0:T(8,128)(2,1)} collective-permute-done((bf16[1024,1024]{1,0:T(8,128)(2,1)}, bf16[1024,1024]{1,0:T(8,128)(2,1)}, u32[]{:S(2)}, u32[]{:S(2)}) %collective-permute-start.5) | collective-permute-done | bytes 2097184 | tf_op jit(solution)/shard_map/cond/branch_0_fun/ppermute | solution.py:32
  357.8 4.1 copy.83
  361.9 0.0 copy-done.5
  361.9 8.0 %fusion.47 = (f32[1024,1024]{0,1:T(8,128)}, bf16[1024,1024]{0,1:T(8,128)(2,1)}) fusion(f32[1024,1024]{1,0:T(8,128)} %get-tuple-element.93, bf16[1,1,512,1024]{3,2,1,0:T(8,128)(2,1)} %all-gather.11.cloned.1.call-done, bf16[512,1024]{1,0:T(8,128)(2,1)S(1)} %copy-done.5, pred[512]{0:T(512)(128)(4,1)S(1)} %compare_and_fusion, ...), kind=kOutput, calls=%fused_computation.71 | convolution fusion | flops 1081606144 | bytes 18874880 | tf_op jit(solution)/shard_map/dot_general | solution.py:57
  370.0 5.5 %copy.59 = f32[1024,2,512]{2,0,1:T(8,128)} copy(f32[1024,2,512]{0,2,1:T(8,128)} %bitcast.122) | data formatting | bytes 8388608 | tf_op jit(solution)/shard_map/reshape | solution.py:39
  375.5 0.0 copy-done.3
  375.5 0.5 multiply_reduce_fusion
  376.0 0.1 reduce_sum.37
  376.1 2.8 divide_convert_fusion
  378.9 1.3 convolution_convert_fusion
  380.2 5.0 %fusion.1 = bf16[1,1024,2,512]{1,3,2,0:T(8,128)(2,1)} fusion(bf16[1024,2,512]{2,0,1:T(8,128)(2,1)S(1)} %divide_convert_fusion, f32[1,1024,2,512]{1,3,2,0:T(8,128)} %bitcast.123, f32[2]{0:T(128)S(1)} %sqrt_add_fusion, bf16[2,512,512]{2,1,0:T(8,128)(2,1)S(1)} %convolution_convert_fusion), kind=kOutput, calls=%fused_computation.5 | convolution fusion | flops 1619525632 | bytes 9437192 | tf_op jit(solution)/shard_map/rizc,rzcd->rizd/dot_general | solution.py:50
  385.2 3.5 fusion.22
  388.8 0.0 copy-start.2
  388.8 6.3 %convert_multiply_fusion = f32[1,1024,2,512]{1,3,2,0:T(8,128)} fusion(bf16[1,1024,2,512]{1,3,2,0:T(8,128)(2,1)} %fusion.1, bf16[2,512,512]{2,1,0:T(8,128)(2,1)S(1)} %fusion.22), kind=kOutput, calls=%fused_computation.20 | convolution fusion | flops 1619525632 | bytes 7340032 | tf_op jit(solution)/shard_map/rizc,rzcd->rizd/dot_general | solution.py:50
  395.1 6.0 %fusion.5 = bf16[1024,1024]{0,1:T(8,128)(2,1)} fusion(f32[1,1024,2,512]{1,3,2,0:T(8,128)} %convert_multiply_fusion, f32[1024,1024]{0,1:T(8,128)} %get-tuple-element.85, bf16[1024,1024]{0,1:T(8,128)(2,1)S(1)} %copy-done.2), kind=kLoop, calls=%fused_computation.13 | loop fusion | flops 5242880 | bytes 12582912 | tf_op jit(solution)/shard_map/convert_element_type | solution.py:96
  401.1 4.1 copy.65
  405.2 2.5 copy.66
  (20 shorter events, 0.1 us)
Async XLA Ops:
  7.2 4.5 %copy-start.8 = (s32[1,2,512]{2,1,0:T(2,128)S(1)}, s32[1,2,512]{2,1,0:T(2,128)}, u32[]{:S(2)}) copy-start(s32[1,2,512]{2,1,0:T(2,128)} %param.18) | copy-start | bytes 12292
  7.2 4.6 %copy-start.7 = (bf16[1,1024,1024]{2,1,0:T(8,128)(2,1)S(1)}, bf16[1,1024,1024]{2,1,0:T(8,128)(2,1)}, u32[]{:S(2)}) copy-start(bf16[1,1024,1024]{2,1,0:T(8,128)(2,1)} %param.15) | copy-start | bytes 6291460
  7.2 205.1 %all-gather.7.cloned.1.call-start = ((), (), s32[]{:S(2)}) async-start(), calls=%async_computation | async-start | bytes 2621440 | tf_op jit(solution)/shard_map/all_gather | solution.py:77
  7.9 211.9 %all-gather.9.cloned.1.call-start = ((), (), s32[]{:S(2)}) async-start(), calls=%async_computation.1 | async-start | bytes 1572864 | tf_op jit(solution)/shard_map/all_gather | solution.py:58
  10.3 351.6 %all-gather.11.cloned.1.call-start = ((), (), s32[]{:S(2)}) async-start(), calls=%async_computation.2 | async-start | bytes 1572864 | tf_op jit(solution)/shard_map/all_gather | solution.py:58
  17.2 4.7 %copy-start.1 = (bf16[1,1024,1024]{1,2,0:T(8,128)(2,1)}, bf16[1,1024,1024]{1,2,0:T(8,128)(2,1)S(1)}, u32[]{:S(2)}) copy-start(bf16[1,1024,1024]{1,2,0:T(8,128)(2,1)S(1)} %copy.38) | copy-start | bytes 6291460
  24.5 140.6 %collective-permute-start.2 = (bf16[1024,1024]{1,0:T(8,128)(2,1)}, bf16[1024,1024]{1,0:T(8,128)(2,1)}, u32[]{:S(2)}, u32[]{:S(2)}) collective-permute-start(bf16[1024,1024]{1,0:T(8,128)(2,1)} %copy.42), channel_id=1, source_target_pairs={{0,16},{16,0},{8,24},{24,8},{1,17},{17,1},{9,25},{25,9},{2,18},{18... | collective-permute-start | bytes 6291464 | tf_op jit(solution)/shard_map/cond/branch_1_fun/ppermute | solution.py:32
  32.5 176.8 %collective-permute-start.3 = (bf16[1024,1024]{1,0:T(8,128)(2,1)}, bf16[1024,1024]{1,0:T(8,128)(2,1)S(1)}, u32[]{:S(2)}, u32[]{:S(2)}) collective-permute-start(bf16[1024,1024]{1,0:T(8,128)(2,1)} %copy.43), channel_id=1, source_target_pairs={{0,16},{16,0},{8,24},{24,8},{1,17},{17,1},{9,25},{25,9},{2,18},{18... | collective-permute-start | bytes 6291464 | tf_op jit(solution)/shard_map/cond/branch_1_fun/ppermute | solution.py:32
  212.3 4.8 %copy-start = (bf16[1,1024,1024]{2,1,0:T(8,128)(2,1)S(1)}, bf16[1,1024,1024]{2,1,0:T(8,128)(2,1)}, u32[]{:S(2)}) copy-start(bf16[1,1024,1024]{2,1,0:T(8,128)(2,1)} %all-gather.7.cloned.1.call-done) | copy-start | bytes 6291460
  238.3 1.3 copy-start.6
  261.6 100.3 %copy-start.5 = (bf16[512,1024]{1,0:T(8,128)(2,1)S(1)}, bf16[512,1024]{1,0:T(8,128)(2,1)}, u32[]{:S(2)}) copy-start(bf16[512,1024]{1,0:T(8,128)(2,1)} %gather_fusion.1) | copy-start | bytes 3145732
  265.7 48.8 %collective-permute-start.4 = (bf16[1024,1024]{1,0:T(8,128)(2,1)}, bf16[1024,1024]{1,0:T(8,128)(2,1)}, u32[]{:S(2)}, u32[]{:S(2)}) collective-permute-start(bf16[1024,1024]{1,0:T(8,128)(2,1)} %copy.53), channel_id=1, source_target_pairs={{0,8},{8,0},{16,24},{24,16},{1,9},{9,1},{17,25},{25,17},{2,10},{10... | collective-permute-start | bytes 6291464 | tf_op jit(solution)/shard_map/cond/branch_0_fun/ppermute | solution.py:32
  269.1 88.7 %collective-permute-start.5 = (bf16[1024,1024]{1,0:T(8,128)(2,1)}, bf16[1024,1024]{1,0:T(8,128)(2,1)}, u32[]{:S(2)}, u32[]{:S(2)}) collective-permute-start(bf16[1024,1024]{1,0:T(8,128)(2,1)} %copy.54), channel_id=1, source_target_pairs={{0,8},{8,0},{16,24},{24,16},{1,9},{9,1},{17,25},{25,17},{2,10},{10... | collective-permute-start | bytes 6291464 | tf_op jit(solution)/shard_map/cond/branch_0_fun/ppermute | solution.py:32
  370.0 5.5 %copy-start.3 = (bf16[1024,1024]{0,1:T(8,128)(2,1)S(1)}, bf16[1024,1024]{0,1:T(8,128)(2,1)}, u32[]{:S(2)}) copy-start(bf16[1024,1024]{0,1:T(8,128)(2,1)} %get-tuple-element.95) | copy-start | bytes 6291460
  388.8 6.3 %copy-start.2 = (bf16[1024,1024]{0,1:T(8,128)(2,1)S(1)}, bf16[1024,1024]{0,1:T(8,128)(2,1)}, u32[]{:S(2)}) copy-start(bf16[1024,1024]{0,1:T(8,128)(2,1)} %fusion.8) | copy-start | bytes 6291460
  401.1 4.1 copy-start.4
Sparse Core Ops, SparseCore 0:
  9.6 25.2 all-gather.6
  36.4 21.2 all-gather.8
  59.3 21.2 all-gather.10
where the time goes:
time: 415 us; the launch traced here: 414 us
  waiting for transfers between devices  257 us (62%)
  local copies, waits for them, and re-layouts  66.2 us (16%)
  matrix products  48.5 us (12%)
  other arithmetic  21.5 us (5%)
  between operations  14.6 us (4%)
  starting transfers between devices  6.12 us (1%)
    ppermute x4, waiting for transfers between devices, partner(): return lax.ppermute(block, axis, route)  256 us
    another operation x8, local copies, waits for them, and re-layouts  28.7 us
    dot_general x4, matrix products, orthogonalize(): jnp.einsum('rizc,rzcd->rizd', iterate, poly, preferred_element_type=jnp.f...  23.2 us
    unnamed x23, local copies, waits for them, and re-layouts  16.8 us
    dot_general x2, matrix products, gradient_at(): lax.dot_general(lax.all_gather(out_grad, 'col', axis=0, tiled=True), chos...  15.7 us
    convert_element_type x2, other arithmetic, body(): own_weights = moved.astype(jnp.bfloat16)  12.7 us
    reshape x2, local copies, waits for them, and re-layouts, orthogonalize(): mixed.astype(jnp.float32)  10.9 us
    dot_general x4, matrix products, orthogonalize(): jnp.einsum('rizc,rizd->rzcd', iterate, iterate, preferred_element_type=jn...  9.59 us
  transfers between devices with their start and end apart: 7, of which 4 were waited for; matrix products, arithmetic and copies ran while one was open for 22% of the time, Pallas kernels for 0%

commit v1 on v0

v1 whole, which is shorter than its diff:
```python
import functools
import math

import jax
import jax.numpy as jnp
from jax import lax
from jax.experimental import pallas as pl
from jax.experimental.pallas import tpu as pltpu
from jax.sharding import PartitionSpec as P


D = 2048
QOUT = 4096
GRID = 4
NS_ITERS = 2
STEPS = 2
SPLIT = 2
NEAR_SHARES = (2, 5, 5, 4)
FAR_SHARES = (5, 5, 4, 2)
TILE = 256

quintic_a = 3.4445
quintic_b = -4.775
quintic_c = 2.0315


f32 = jnp.float32
bf16 = jnp.bfloat16
dot = functools.partial(jnp.dot, preferred_element_type=f32)


def xor_route(count, mask):
    return [(low, low ^ mask) for low in range(count) if low ^ mask < count]


def send(x, axis, route):
    return lax.ppermute(x, axis, route)


def gather_pieces(x, axis):
    count = lax.axis_size(axis)
    here = lax.axis_index(axis)
    if count & (count - 1):
        whole = lax.all_gather(x, axis, axis=0)
        return [whole[k] for k in range(count)], [jnp.int32(k) for k in range(count)]
    pieces = {0: x}
    mask = count >> 1
    while mask:
        for k, piece in list(pieces.items()):
            pieces[k ^ mask] = send(piece, axis, xor_route(count, mask))
        mask >>= 1
    return [pieces[k] for k in range(count)], [here ^ k for k in range(count)]


def tt(x, y):
    return lax.dot_general(x, y, (((0,), (0,)), ((), ())), preferred_element_type=f32)


def newton_schulz(x_ref, block):
    norm = jnp.sqrt(jnp.sum(block * block)) + 1e-07
    x_ref[...] = (block / norm).astype(bf16)
    lax.fori_loop(0, NS_ITERS, lambda turn, _: newton_schulz_turn(x_ref), None)


def newton_schulz_turn(x_ref):
    x = x_ref[...]
    gram = tt(x, x).astype(bf16)
    poly = (quintic_b * gram.astype(f32) + quintic_c * dot(gram, gram)).astype(bf16)
    x_ref[...] = (quintic_a * x.astype(f32) + dot(x, poly)).astype(bf16)


def call(kernel, out_shape, mib=16, **kw):
    params = pltpu.CompilerParams(vmem_limit_bytes=mib << 20)
    return pl.pallas_call(kernel, out_shape=out_shape, compiler_params=params, **kw)


def loop(count, step):
    lax.fori_loop(0, count, lambda k, _: step(k), None)


def tile(k, size):
    return pl.ds(pl.multiple_of(k * size, size), size)


def prepare(pool_pieces, pool_bases, grad_pieces, token_ids, step):
    count_p, count_g = len(pool_pieces), len(grad_pieces)
    pool_rows, cols = pool_pieces[0].shape
    tokens, rows = grad_pieces[0].shape
    total = count_g * tokens

    def kernel(base_ref, ids_ref, *refs):
        pools, grads, (chosen_ref, turned_ref) = refs[:count_p], refs[count_p:-2], refs[-2:]
        lane = lax.broadcasted_iota(jnp.int32, (tokens, pool_rows), 1)

        def pick(g):
            here = tile(g, tokens)
            own = ids_ref[here, :]
            acc = jnp.zeros((tokens, cols), f32)
            for k in range(count_p):
                hot = jnp.where(own - base_ref[k] == lane, 1.0, 0.0).astype(bf16)
                acc += dot(hot, pools[k][...])
            chosen_ref[here, :] = acc.astype(bf16)

        loop(count_g, pick)
        for g in range(count_g):
            turned_ref[:, g * tokens : (g + 1) * tokens] = grads[g][...].T

    whole = lambda *shape: pl.BlockSpec(shape, lambda i: (0,) * len(shape))
    return call(
        kernel,
        (jax.ShapeDtypeStruct((total, cols), bf16), jax.ShapeDtypeStruct((rows, total), bf16)),
        grid=(1,),
        in_specs=[pl.BlockSpec(memory_space=pltpu.SMEM), pl.BlockSpec((total, 1), lambda i: (step, 0))]
        + [whole(pool_rows, cols)] * count_p
        + [whole(tokens, rows)] * count_g,
        out_specs=(whole(total, cols), whole(rows, total)),
    )(pool_bases, token_ids, *pool_pieces, *grad_pieces)


def first_mix(own, other, older, turned, chosen, row, col, height, width):
    def kernel(own_ref, other_ref, older_ref, turned_ref, chosen_ref, out_ref):
        def mix(k):
            t = tile(k, TILE)
            fresh = dot(turned_ref[t, :], chosen_ref[...])
            mean = 0.5 * (own_ref[t, :].astype(f32) + other_ref[t, :].astype(f32))
            out_ref[t, :] = (mean + fresh - older_ref[t, :].astype(f32)).astype(bf16)

        loop(height // TILE, mix)

    tokens = chosen.shape[0]
    piece = pl.BlockSpec((height, width), lambda i: (row, col))
    alone = pl.BlockSpec((height, width), lambda i: (0, 0))
    return call(
        kernel,
        jax.ShapeDtypeStruct((height, width), bf16),
        grid=(1,),
        in_specs=[
            piece,
            alone,
            piece,
            pl.BlockSpec((height, tokens), lambda i: (row, 0)),
            pl.BlockSpec((tokens, width), lambda i: (0, col)),
        ],
        out_specs=alone,
    )(own, other, older, turned, chosen)


def stacked(refs):
    return jnp.concatenate([r[...] for r in refs], axis=0)


def newton_schulz(x_ref, count):
    def scale(k):
        block = x_ref[k].astype(f32)
        norm = jnp.sqrt(jnp.sum(block * block)) + 1e-07
        x_ref[k] = (block * (1.0 / norm)).astype(bf16)
        loop(NS_ITERS, lambda _: turn(k))

    def turn(k):
        x = x_ref[k]
        gram = tt(x, x).astype(bf16)
        poly = (quintic_b * gram.astype(f32) + quintic_c * dot(gram, gram)).astype(bf16)
        x_ref[k] = (quintic_a * x.astype(f32) + dot(x, poly)).astype(bf16)

    loop(count, scale)


def orthogonal(blocks):
    pieces = len(blocks[0])
    height, width = blocks[0][0].shape
    height *= pieces

    def kernel(*refs):
        x_ref = refs[-1]
        for k in range(len(blocks)):
            x_ref[k] = stacked(refs[k * pieces : (k + 1) * pieces])
        newton_schulz(x_ref, len(blocks))

    return call(
        kernel, jax.ShapeDtypeStruct((len(blocks), height, width), bf16)
    )(*[piece for block in blocks for piece in block])


def second_mix(mine, theirs, grads, row, col, whole, previous):
    pieces = len(mine)
    height, width = mine[0].shape
    height *= pieces

    def kernel(*refs):
        mine_refs, theirs_refs = refs[:pieces], refs[pieces : 2 * pieces]
        turned_1, chosen_1, turned_0, chosen_0 = refs[2 * pieces : 2 * pieces + 4]
        tracker_ref, update_ref, x_ref, y_ref = refs[-4:]
        x_ref[0] = stacked(theirs_refs)
        y_ref[...] = stacked(mine_refs)

        def mix(k):
            t = tile(k, TILE)
            fresh = dot(turned_1[t, :], chosen_1[...]) - dot(turned_0[t, :], chosen_0[...])
            mean = 0.5 * (y_ref[t, :].astype(f32) + x_ref[0, t, :].astype(f32))
            mixed = (mean + fresh).astype(bf16)
            tracker_ref[t, :] = mixed
            x_ref[1, t, :] = mixed

        loop(height // TILE, mix)
        newton_schulz(x_ref, 2)
        update_ref[...] = 0.5 * x_ref[0].astype(f32) + x_ref[1].astype(f32)

    alone = pl.BlockSpec((height // pieces, width), lambda i: (0, 0))
    operands = [*mine, *theirs, *grads]
    in_specs = [alone] * (2 * pieces)
    for turned, chosen in zip(grads[::2], grads[1::2]):
        in_specs += [pl.BlockSpec((height, turned.shape[1]), lambda i: (row, 0))]
        in_specs += [pl.BlockSpec((chosen.shape[0], width), lambda i: (0, col))]
    aliases = {}
    if previous is not None:
        aliases = {len(operands): 0}
        operands += [previous]
        in_specs += [pl.BlockSpec(memory_space=pl.ANY)]
    return call(
        kernel,
        mib=32,
        out_shape=(jax.ShapeDtypeStruct((1, *whole), bf16), jax.ShapeDtypeStruct((height, width), f32)),
        grid=(1,),
        in_specs=in_specs,
        out_specs=(
            pl.BlockSpec((None, height, width), lambda i: (0, row, col)),
            pl.BlockSpec((height, width), lambda i: (0, 0)),
        ),
        scratch_shapes=[pltpu.VMEM((2, height, width), bf16), pltpu.VMEM((height, width), bf16)],
        input_output_aliases=aliases,
    )(*operands)


def apply(means, first, updates, scale, at, blocks, whole, previous):
    rows, cols = means[0].shape
    _, height, width = first.shape
    unit = math.gcd(at, rows) if at else rows
    steps = rows // unit

    def kernel(*refs):
        mean_refs, (first_ref, *update_refs) = refs[: len(means)], refs[len(means) : len(operands)]
        out_ref = refs[-1]
        for c in range(blocks):
            cut = slice(c * width, (c + 1) * width)
            mean = sum(r[:, cut].astype(f32) for r in mean_refs)
            update = 0.5 * first_ref[c].astype(f32) + update_refs[c][...]
            out_ref[:, cut] = (mean - scale * update).astype(bf16)

    row = at // height
    into = lambda i: (at % height) // unit + i
    operands = [*means, first, *updates[row * blocks : (row + 1) * blocks]]
    in_specs = [pl.BlockSpec((unit, cols), lambda i: (i, 0))] * len(means)
    in_specs += [pl.BlockSpec((blocks, unit, width), lambda i: (row, into(i), 0))]
    in_specs += [pl.BlockSpec((unit, width), lambda i: (into(i), 0))] * blocks
    aliases = {}
    if previous is not None:
        aliases = {len(operands): 0}
    call_operands = operands + ([previous] if previous is not None else [])
    return call(
        kernel,
        jax.ShapeDtypeStruct((1, *whole), bf16),
        grid=(steps,),
        in_specs=in_specs + [pl.BlockSpec(memory_space=pl.ANY)] * len(aliases),
        out_specs=pl.BlockSpec((None, unit, cols), lambda i: (0, at // unit + i, 0)),
        input_output_aliases=aliases,
    )(*call_operands)


def mean_of_four(own, first_route, second_route):
    count = lax.axis_size("rep")

    def both(x, y, factor):
        return (factor * (x.astype(f32) + y.astype(f32))).astype(bf16)

    if count != 4:
        partial = both(own, send(own, "rep", first_route), 1.0)
        across = send(partial, "rep", second_route)
        return [both(partial, across, 0.25)]
    place = lax.axis_index("rep")
    inner = (place == 1) | (place == 2)
    partial = both(own, send(own, "rep", [(0, 1), (3, 2)]), 1.0)
    across = send(partial, "rep", [(1, 2), (2, 1)])
    mean = both(partial, across, jnp.where(inner, 0.25, 0.0))
    return [mean, send(mean, "rep", [(1, 0), (2, 3)])]


def two_steps(first_mask, second_mask, weights, tracker, grad_prev, pool, out_grads, row_ids):
    count = lax.axis_size("rep")
    rows, cols = weights.shape
    height, width = QOUT // GRID, D // GRID
    piece = height // SPLIT
    scale = 0.2 * math.sqrt(QOUT // GRID)
    first_route, second_route = xor_route(count, first_mask), xor_route(count, second_mask)

    tokens = out_grads.shape[1]
    pool_pieces, pool_from = gather_pieces(pool, "row")
    pool_bases = jnp.stack(pool_from).astype(jnp.int32) * pool.shape[0]
    grad_pieces = []
    for step in range(STEPS):
        pieces, grad_from = gather_pieces(out_grads[step], "col")
        grad_pieces.append(pieces)
    ids = [
        lax.dynamic_slice(row_ids, (step, place * tokens), (1, tokens))
        for step in range(STEPS)
        for place in grad_from
    ]
    ids = jnp.concatenate(ids, axis=1).reshape(-1, 1)
    grads = []
    for step in range(STEPS):
        chosen, turned = prepare(pool_pieces, pool_bases, grad_pieces[step], ids, step)
        grads = [turned, chosen, *grads]

    def part(x, r, c):
        return lax.slice(x, (r * piece, c * width), ((r + 1) * piece, (c + 1) * width))

    blocks = [(r, c) for r in range(rows // height) for c in range(cols // width)]
    mine, theirs = [], []
    for row, col in blocks:
        mine.append([])
        theirs.append([])
        for s in range(SPLIT):
            r = row * SPLIT + s
            other = send(part(tracker, r, col), "rep", first_route)
            mixed = first_mix(tracker, other, grad_prev, *grads[2:], r, col, piece, width)
            mine[-1].append(mixed)
            theirs[-1].append(send(mixed, "rep", second_route))
    first = orthogonal(mine)
    new_tracker, updates = None, []
    for b, (row, col) in enumerate(blocks):
        new_tracker, update = second_mix(
            mine[b], theirs[b], grads, row, col, weights.shape, new_tracker
        )
        updates.append(update)

    new_weights, at = None, 0
    shares = NEAR_SHARES if first_mask == 1 else FAR_SHARES
    for share in shares:
        size = rows * share // sum(shares)
        own = lax.optimization_barrier(lax.slice_in_dim(weights, at, at + size))
        means = mean_of_four(own, first_route, second_route)
        new_weights = apply(
            means, first, updates, scale, at, cols // width, weights.shape, new_weights
        )
        at += size
    return new_weights, new_tracker


def body(weights, tracker, grad_prev, pool, out_grads, row_ids, step_index):
    levels = lax.axis_size("rep").bit_length() - 1

    def branch(level, *args):
        return two_steps(1 << level, 1 << (level + 1) % levels, *args)

    return lax.switch(
        step_index[0] % levels,
        [functools.partial(branch, level) for level in range(levels)],
        weights[0],
        tracker[0],
        grad_prev[0],
        pool[0],
        out_grads[0],
        row_ids[0],
    )


def solution(mesh):
    in_specs = (
        P("rep", "row", "col"),
        P("rep", "row", "col"),
        P("rep", "row", "col"),
        P("rep", "row", "col"),
        P("rep", None, "col", "row"),
        P("rep", None, None),
        P(),
    )
    out_specs = (P("rep", "row", "col"), P("rep", "row", "col"))
    return jax.shard_map(body, mesh=mesh, in_specs=in_specs, out_specs=out_specs, check_vma=False)
```

time: 415 us -> 264 us (0.64)
  waiting for transfers between devices: 257 us -> 160 us
  local copies, waits for them, and re-layouts: 66.2 us -> 7.58 us
  matrix products: 48.5 us -> 0 us
  Pallas kernels: 0 us -> 46.6 us
  starting transfers between devices: 6.12 us -> 40.9 us
  other arithmetic: 21.5 us -> 6.55 us
  between operations: 14.6 us -> 1.29 us
    ppermute x4 -> x25, waiting for transfers between devices: 256 us -> 160 us  [send(): return lax.ppermute(x, axis, route)]
    dot_general x10 -> x0, matrix products: 48.5 us -> none  [the longest x4 23.2 us: orthogonalize(): jnp.einsum('rizc,rzcd->rizd', iterate, poly, preferred_element_type=jnp.f...]
    pallas_call x0 -> x13, Pallas kernels: none -> 46.6 us  [the longest x2 22.1 us: second_mix(): call(kernel, mib=32, out_shape=(jax.ShapeDtypeStruct((1, *whole), bf16),...]
    ppermute x4 -> x25, starting transfers between devices: 6 us -> 40.9 us  [send(): return lax.ppermute(x, axis, route)]
    another operation x8 -> x0, local copies, waits for them, and re-layouts: 28.7 us -> none
    unnamed x23 -> x2, local copies, waits for them, and re-layouts: 16.8 us -> 1.32 us
    convert_element_type x5 -> x8, other arithmetic: 20.7 us -> 6.46 us  [both(): return (factor * (x.astype(f32) + y.astype(f32))).astype(bf16)]
    reshape x2 -> x1, local copies, waits for them, and re-layouts: 10.9 us -> 0.22 us  [two_steps(): ids = jnp.concatenate(ids, axis=1).reshape(-1, 1)]
  transfers between devices with their start and end apart: 7 -> 25, of which waited for: 4 -> 9; matrix products, arithmetic and copies ran while one was open for 22% -> 4% of each run, Pallas kernels for 0% -> 17%
where the time goes in v1:
time: 264 us; the launch traced here: 263 us
  waiting for transfers between devices  160 us (61%)
  Pallas kernels  46.6 us (18%)
  starting transfers between devices  40.9 us (15%)
  local copies, waits for them, and re-layouts  7.58 us (3%)
  other arithmetic  6.55 us (2%)
    ppermute x25, waiting for transfers between devices, send(): return lax.ppermute(x, axis, route)  160 us
    ppermute x25, starting transfers between devices, send(): return lax.ppermute(x, axis, route)  40.9 us
    pallas_call x2, Pallas kernels, second_mix(): call(kernel, mib=32, out_shape=(jax.ShapeDtypeStruct((1, *whole), bf16),...  22.1 us
    pallas_call x1, Pallas kernels, orthogonal(): call(kernel, jax.ShapeDtypeStruct((len(blocks), height, width), bf16))  8.89 us
    convert_element_type x8, other arithmetic, both(): return (factor * (x.astype(f32) + y.astype(f32))).astype(bf16)  6.46 us
    pallas_call x4, Pallas kernels, apply(): call(kernel, jax.ShapeDtypeStruct((1, *whole), bf16), grid=(steps,), in_s...  6.42 us
    pallas_call x2, Pallas kernels, prepare(): call(kernel, (jax.ShapeDtypeStruct((total, cols), bf16), jax.ShapeDtypeSt...  6.08 us
  transfers between devices with their start and end apart: 25, of which 9 were waited for; matrix products, arithmetic and copies ran while one was open for 4% of the time, Pallas kernels for 17%

profile of v1, /device:TPU:0, one launch (start us, length us, event | category | flops | bytes accessed | tf_op | source)
XLA Modules:
  0.0 263.2 jit_solution(13578172070410318928)
XLA Ops:
  1.3 260.6 %conditional.1 = (bf16[1,1024,1024]{2,1,0:T(8,128)(2,1)S(1)}, bf16[1,1024,1024]{2,1,0:T(8,128)(2,1)}) conditional(s32[]{:T(128)} %clamp.3, (bf16[1024,1024]{1,0:T(8,128)(2,1)}, bf16[1024,1024]{1,0:T(8,128)(2,1)}, s32[2,512]{1,0:T(2,128)}, bf16[256,1024]{1,0:T(8,128)(2,1)}, bf16[2,256,1024]{2,1,0:T(8,128)(2,1)}, ...), branch_computations={%region_0.1_spmd, %region_1.2_spmd} | conditional | flops 9440296 | bytes 127968856 | solution.py:354
  1.3 0.0 copy-start.4
  1.3 2.8 %fusion.1 = (bf16[512,512]{1,0:T(8,128)(2,1)}, bf16[512,512]{1,0:T(8,128)(2,1)}, bf16[512,512]{1,0:T(8,128)(2,1)S(1)}, bf16[512,512]{1,0:T(8,128)(2,1)}) fusion(bf16[1024,1024]{1,0:T(8,128)(2,1)} %get-tuple-element.25.own_ref), kind=kLoop, calls=%fused_computation.33 | loop fusion | bytes 4194304 | tf_op jit(solution)/shard_map/cond/branch_0_fun/slice | solution.py:314
  4.1 3.1 %collective-permute-start.9 = (bf16[512,512]{1,0:T(8,128)(2,1)S(1)}, bf16[512,512]{1,0:T(8,128)(2,1)S(1)}, u32[]{:S(2)}, u32[]{:S(2)}) collective-permute-start(bf16[512,512]{1,0:T(8,128)(2,1)S(1)} %get-tuple-element.59), channel_id=1, source_target_pairs={{0,8},{8,0},{16,24},{24,16},{1,9},{9,1},{17,25},{25,17},{2,10},{10... | collective-permute-start | bytes 1572872 | tf_op jit(solution)/shard_map/cond/branch_0_fun/ppermute | solution.py:37
  7.2 1.5 collective-permute-start.5
  8.7 1.1 fusion
  9.9 3.2 %collective-permute-start.16 = (bf16[320,1024]{1,0:T(8,128)(2,1)}, bf16[320,1024]{1,0:T(8,128)(2,1)}, u32[]{:S(2)}, u32[]{:S(2)}) collective-permute-start(bf16[320,1024]{1,0:T(8,128)(2,1)} %get-tuple-element.56), channel_id=1, source_target_pairs={{0,8},{24,16},{1,9},{25,17},{2,10},{26,18},{3,11},{27,19},{4,12},{... | collective-permute-start | bytes 1966088 | tf_op jit(solution)/shard_map/cond/branch_0_fun/ppermute | solution.py:37
  13.1 2.2 collective-permute-start.19
  15.2 2.0 collective-permute-start.22
  17.2 0.1 slice_bitcast_fusion
  17.3 1.9 slice.40
  19.2 32.9 %collective-permute-done.22 = bf16[128,1024]{1,0:T(8,128)(2,1)} collective-permute-done((bf16[128,1024]{1,0:T(8,128)(2,1)S(1)}, bf16[128,1024]{1,0:T(8,128)(2,1)}, u32[]{:S(2)}, u32[]{:S(2)}) %collective-permute-start.22) | collective-permute-done | bytes 262176 | tf_op jit(solution)/shard_map/cond/branch_0_fun/ppermute | solution.py:37
  52.1 1.5 collective-permute-start.7
  53.6 5.3 %collective-permute-start = (bf16[256,1024]{1,0:T(8,128)(2,1)}, bf16[256,1024]{1,0:T(8,128)(2,1)}, u32[]{:S(2)}, u32[]{:S(2)}) collective-permute-start(bf16[256,1024]{1,0:T(8,128)(2,1)} %slice.40), channel_id=1, source_target_pairs={{0,8},{24,16},{1,9},{25,17},{2,10},{26,18},{3,11},{27,19},{4,12},{... | collective-permute-start | bytes 1572872 | tf_op jit(solution)/shard_map/cond/branch_0_fun/ppermute | solution.py:37
  58.9 0.1 constant_dynamic-slice_fusion.1
  59.0 0.2 copy.19.ids_ref
  59.2 0.1 add_multiply_fusion.base_ref
  59.3 0.0 collective-permute-start.6
  59.4 1.6 add_convert_fusion.1
  61.0 0.1 collective-permute-start.10
  61.1 5.5 %collective-permute-done.7.refs_5_ = bf16[256,1024]{1,0:T(8,128)(2,1)} collective-permute-done((bf16[256,1024]{1,0:T(8,128)(2,1)S(1)}, bf16[256,1024]{1,0:T(8,128)(2,1)}, u32[]{:S(2)}, u32[]{:S(2)}) %collective-permute-start.7) | collective-permute-done | bytes 524320 | tf_op jit(solution)/shard_map/cond/branch_0_fun/ppermute | solution.py:37
  66.5 2.6 collective-permute-start.3
  69.1 1.6 collective-permute-done
  70.7 2.5 collective-permute-start.8
  73.2 0.7 collective-permute-start.17
  73.9 1.5 add_convert_fusion
  75.4 0.7 collective-permute-start.20
  76.1 1.0 add_convert_fusion.3
  77.2 1.5 add_convert_fusion.2
  78.7 3.2 %branch_0_fun.13 = (bf16[512,1024]{1,0:T(8,128)(2,1)S(1)}, bf16[1024,512]{1,0:T(8,128)(2,1)S(1)}) custom-call(s32[4]{0:T(128)S(1)} %add_multiply_fusion.base_ref, s32[1024,1]{1,0:T(8,128)S(1)} %copy.19.ids_ref, bf16[256,1024]{1,0:T(8,128)(2,1)} %get-tuple-element.28.refs_0_, bf16[256,1024]{1,0:T(8,128)(2,1)S(1)} %collective-permute-done.4.refs_1_, ...), custom_call_target="tpu_custom_call" | custom-call | tf_op jit(solution)/shard_map/cond/branch_0_fun/pallas_call | solution.py:109
  81.9 0.8 branch_0_fun.16.refs_2_.refs_0_
  82.7 0.6 collective-permute-start.13
  83.3 0.8 branch_0_fun.17.refs_3_.refs_1_
  84.1 9.0 %collective-permute-done.3.other_ref = bf16[512,512]{1,0:T(8,128)(2,1)S(1)} collective-permute-done((bf16[512,512]{1,0:T(8,128)(2,1)S(1)}, bf16[512,512]{1,0:T(8,128)(2,1)S(1)}, u32[]{:S(2)}, u32[]{:S(2)}) %collective-permute-start.3) | collective-permute-done | bytes 524320 | tf_op jit(solution)/shard_map/cond/branch_0_fun/ppermute | solution.py:37
  93.0 0.7 collective-permute-start.23
  93.7 0.8 branch_0_fun.14.refs_0_
  94.5 9.1 %collective-permute-done.8.other_ref = bf16[512,512]{1,0:T(8,128)(2,1)S(1)} collective-permute-done((bf16[512,512]{1,0:T(8,128)(2,1)S(1)}, bf16[512,512]{1,0:T(8,128)(2,1)S(1)}, u32[]{:S(2)}, u32[]{:S(2)}) %collective-permute-start.8) | collective-permute-done | bytes 524320 | tf_op jit(solution)/shard_map/cond/branch_0_fun/ppermute | solution.py:37
  103.5 0.7 collective-permute-start.1
  104.2 0.8 branch_0_fun.15.refs_1_
  105.0 5.2 %collective-permute-start.14 = (bf16[512,512]{1,0:T(8,128)(2,1)S(1)}, bf16[512,512]{1,0:T(8,128)(2,1)S(1)}, u32[]{:S(2)}, u32[]{:S(2)}) collective-permute-start(bf16[512,512]{1,0:T(8,128)(2,1)S(1)} %branch_0_fun.16.refs_2_.refs_0_), channel_id=1, source_target_pairs={{0,16},{8,24},{16,0},{24,8},{1,17},{9,25},{17,1},{25,9},{2,18},{10... | collective-permute-start | bytes 1572872 | tf_op jit(solution)/shard_map/cond/branch_0_fun/ppermute | solution.py:37
  110.2 0.2 multiply_convert_fusion.1.refs_0_
  110.5 0.1 collective-permute-start.11
  110.6 0.2 multiply_convert_fusion.refs_0_
  110.8 3.0 %collective-permute-start.15 = (bf16[512,512]{1,0:T(8,128)(2,1)S(1)}, bf16[512,512]{1,0:T(8,128)(2,1)S(1)}, u32[]{:S(2)}, u32[]{:S(2)}) collective-permute-start(bf16[512,512]{1,0:T(8,128)(2,1)S(1)} %branch_0_fun.17.refs_3_.refs_1_), channel_id=1, source_target_pairs={{0,16},{8,24},{16,0},{24,8},{1,17},{9,25},{17,1},{25,9},{2,18},{10... | collective-permute-start | bytes 1572872 | tf_op jit(solution)/shard_map/cond/branch_0_fun/ppermute | solution.py:37
  113.8 0.1 collective-permute-start.12
  113.9 1.3 collective-permute-start.18
  115.2 63.2 %collective-permute-done.14.refs_2_ = bf16[512,512]{1,0:T(8,128)(2,1)S(1)} collective-permute-done((bf16[512,512]{1,0:T(8,128)(2,1)S(1)}, bf16[512,512]{1,0:T(8,128)(2,1)S(1)}, u32[]{:S(2)}, u32[]{:S(2)}) %collective-permute-start.14) | collective-permute-done | bytes 524320 | tf_op jit(solution)/shard_map/cond/branch_0_fun/ppermute | solution.py:37
  178.4 1.3 collective-permute-start.21
  179.7 0.2 multiply_convert_fusion.2.refs_0_
  179.9 9.7 %collective-permute-done.11.refs_2_ = bf16[512,512]{1,0:T(8,128)(2,1)S(1)} collective-permute-done((bf16[512,512]{1,0:T(8,128)(2,1)S(1)}, bf16[512,512]{1,0:T(8,128)(2,1)S(1)}, u32[]{:S(2)}, u32[]{:S(2)}) %collective-permute-start.11) | collective-permute-done | bytes 524320 | tf_op jit(solution)/shard_map/cond/branch_0_fun/ppermute | solution.py:37
  189.7 1.3 collective-permute-start.2
  190.9 0.1 multiply_convert_fusion.3.refs_0_
  191.0 19.6 %collective-permute-done.12.refs_3_ = bf16[512,512]{1,0:T(8,128)(2,1)S(1)} collective-permute-done((bf16[512,512]{1,0:T(8,128)(2,1)S(1)}, bf16[512,512]{1,0:T(8,128)(2,1)S(1)}, u32[]{:S(2)}, u32[]{:S(2)}) %collective-permute-start.12) | collective-permute-done | bytes 524320 | tf_op jit(solution)/shard_map/cond/branch_0_fun/ppermute | solution.py:37
  210.7 1.5 collective-permute-start.24
  212.1 8.9 %branch_0_fun.18.refs_2_ = bf16[2,1024,512]{2,1,0:T(8,128)(2,1)S(1)} custom-call(bf16[512,512]{1,0:T(8,128)(2,1)S(1)} %branch_0_fun.14.refs_0_, bf16[512,512]{1,0:T(8,128)(2,1)S(1)} %branch_0_fun.15.refs_1_, bf16[512,512]{1,0:T(8,128)(2,1)S(1)} %branch_0_fun.16.refs_2_.refs_0_, bf16[512,512]{1,0:T(8,128)(2,1)S(1)} %branch_0_fun.17.refs_3_.refs_1_), custom_call_target="tpu_custom_call" | custom-call | tf_op jit(solution)/shard_map/cond/branch_0_fun/pallas_call | solution.py:179
  221.0 2.9 %branch_0_fun.19 = (bf16[512,1024]{1,0:T(8,128)(2,1)S(1)}, bf16[1024,512]{1,0:T(8,128)(2,1)S(1)}) custom-call(s32[4]{0:T(128)S(1)} %add_multiply_fusion.base_ref, s32[1024,1]{1,0:T(8,128)S(1)} %copy.19.ids_ref, bf16[256,1024]{1,0:T(8,128)(2,1)} %get-tuple-element.28.refs_0_, bf16[256,1024]{1,0:T(8,128)(2,1)S(1)} %collective-permute-done.4.refs_1_, ...), custom_call_target="tpu_custom_call" | custom-call | tf_op jit(solution)/shard_map/cond/branch_0_fun/pallas_call | solution.py:109
  223.9 11.1 %branch_0_fun.20 = (bf16[1,1024,1024]{2,1,0:T(8,128)(2,1)S(1)}, f32[1024,512]{1,0:T(8,128)S(1)}) custom-call(bf16[512,512]{1,0:T(8,128)(2,1)S(1)} %branch_0_fun.14.refs_0_, bf16[512,512]{1,0:T(8,128)(2,1)S(1)} %branch_0_fun.15.refs_1_, bf16[512,512]{1,0:T(8,128)(2,1)S(1)} %collective-permute-done.11.refs_2_, ...), custom_call_target="tpu_custom_call" | custom-call | tf_op jit(solution)/shard_map/cond/branch_0_fun/pallas_call | solution.py:219
  235.0 11.1 %branch_0_fun.21 = (bf16[1,1024,1024]{2,1,0:T(8,128)(2,1)S(1)}, f32[1024,512]{1,0:T(8,128)S(1)}) custom-call(bf16[512,512]{1,0:T(8,128)(2,1)S(1)} %branch_0_fun.16.refs_2_.refs_0_, bf16[512,512]{1,0:T(8,128)(2,1)S(1)} %branch_0_fun.17.refs_3_.refs_1_, bf16[512,512]{1,0:T(8,128)(2,1)S(1)} %collective-permute-done.14.refs_2_, ...), custom_call_target="tpu_custom_call", output_to_operand_aliasing={{0}: (8, {})} | custom-call | tf_op jit(solution)/shard_map/cond/branch_0_fun/pallas_call | solution.py:219
  246.1 9.3 %collective-permute-done.24.refs_1_ = bf16[128,1024]{1,0:T(8,128)(2,1)S(1)} collective-permute-done((bf16[128,1024]{1,0:T(8,128)(2,1)S(1)}, bf16[128,1024]{1,0:T(8,128)(2,1)S(1)}, u32[]{:S(2)}, u32[]{:S(2)}) %collective-permute-start.24) | collective-permute-done | bytes 262176 | tf_op jit(solution)/shard_map/cond/branch_0_fun/ppermute | solution.py:37
  255.4 0.8 branch_0_fun.22.refs_5_
  256.3 2.2 branch_0_fun.23.refs_5_
  258.5 2.2 branch_0_fun.24.refs_5_
  260.8 1.1 branch_0_fun.25
  261.9 1.3 copy-done.8
  (35 shorter events, 0.1 us)
Async XLA Ops:
  1.3 7.4 %copy-start.4 = (bf16[1024,1024]{1,0:T(8,128)(2,1)S(1)}, bf16[1024,1024]{1,0:T(8,128)(2,1)}, u32[]{:S(2)}) copy-start(bf16[1024,1024]{1,0:T(8,128)(2,1)} %get-tuple-element.24) | copy-start | bytes 6291460 | tf_op jit(solution)/shard_map/cond
  4.1 47.9 %collective-permute-start.9 = (bf16[512,512]{1,0:T(8,128)(2,1)S(1)}, bf16[512,512]{1,0:T(8,128)(2,1)S(1)}, u32[]{:S(2)}, u32[]{:S(2)}) collective-permute-start(bf16[512,512]{1,0:T(8,128)(2,1)S(1)} %get-tuple-element.59), channel_id=1, source_target_pairs={{0,8},{8,0},{16,24},{24,16},{1,9},{9,1},{17,25},{25,17},{2,10},{10... | collective-permute-start | bytes 1572872 | tf_op jit(solution)/shard_map/cond/branch_0_fun/ppermute | solution.py:37
  7.2 46.4 %collective-permute-start.5 = (bf16[256,1024]{1,0:T(8,128)(2,1)}, bf16[256,1024]{1,0:T(8,128)(2,1)S(1)}, u32[]{:S(2)}, u32[]{:S(2)}) collective-permute-start(bf16[256,1024]{1,0:T(8,128)(2,1)} %get-tuple-element.28.refs_0_), channel_id=1, source_target_pairs={{0,4},{2,6},{4,0},{6,2},{1,5},{3,7},{5,1},{7,3},{8,12},{10,14},{12... | collective-permute-start | bytes 1572872 | tf_op jit(solution)/shard_map/cond/branch_0_fun/ppermute | solution.py:37
  8.7 8.5 %copy-start.9 = (bf16[2,256,1024]{2,1,0:T(8,128)(2,1)S(1)}, bf16[2,256,1024]{2,1,0:T(8,128)(2,1)}, u32[]{:S(2)}) copy-start(bf16[2,256,1024]{2,1,0:T(8,128)(2,1)} %get-tuple-element.29) | copy-start | bytes 3145732 | tf_op jit(solution)/shard_map/cond
  9.9 49.5 %collective-permute-start.16 = (bf16[320,1024]{1,0:T(8,128)(2,1)}, bf16[320,1024]{1,0:T(8,128)(2,1)}, u32[]{:S(2)}, u32[]{:S(2)}) collective-permute-start(bf16[320,1024]{1,0:T(8,128)(2,1)} %get-tuple-element.56), channel_id=1, source_target_pairs={{0,8},{24,16},{1,9},{25,17},{2,10},{26,18},{3,11},{27,19},{4,12},{... | collective-permute-start | bytes 1966088 | tf_op jit(solution)/shard_map/cond/branch_0_fun/ppermute | solution.py:37
  13.1 60.1 %collective-permute-start.19 = (bf16[320,1024]{1,0:T(8,128)(2,1)}, bf16[320,1024]{1,0:T(8,128)(2,1)}, u32[]{:S(2)}, u32[]{:S(2)}) collective-permute-start(bf16[320,1024]{1,0:T(8,128)(2,1)} %get-tuple-element.55), channel_id=1, source_target_pairs={{0,8},{24,16},{1,9},{25,17},{2,10},{26,18},{3,11},{27,19},{4,12},{... | collective-permute-start | bytes 1966088 | tf_op jit(solution)/shard_map/cond/branch_0_fun/ppermute | solution.py:37
  15.2 36.8 %collective-permute-start.22 = (bf16[128,1024]{1,0:T(8,128)(2,1)S(1)}, bf16[128,1024]{1,0:T(8,128)(2,1)}, u32[]{:S(2)}, u32[]{:S(2)}) collective-permute-start(bf16[128,1024]{1,0:T(8,128)(2,1)S(1)} %slice.49), channel_id=1, source_target_pairs={{0,8},{24,16},{1,9},{25,17},{2,10},{26,18},{3,11},{27,19},{4,12},{... | collective-permute-start | bytes 786440 | tf_op jit(solution)/shard_map/cond/branch_0_fun/ppermute | solution.py:37
  17.2 41.7 %copy-start.17 = (s32[2,512]{1,0:T(2,128)S(1)}, s32[2,512]{1,0:T(2,128)}, u32[]{:S(2)}) copy-start(s32[2,512]{1,0:T(2,128)} %get-tuple-element.27) | copy-start | bytes 12292 | tf_op jit(solution)/shard_map/cond
  52.1 8.9 %collective-permute-start.4 = (bf16[256,1024]{1,0:T(8,128)(2,1)}, bf16[256,1024]{1,0:T(8,128)(2,1)S(1)}, u32[]{:S(2)}, u32[]{:S(2)}) collective-permute-start(bf16[256,1024]{1,0:T(8,128)(2,1)} %get-tuple-element.28.refs_0_), channel_id=1, source_target_pairs={{0,2},{2,0},{4,6},{6,4},{1,3},{3,1},{5,7},{7,5},{8,10},{10,8},{12,... | collective-permute-start | bytes 1572872 | tf_op jit(solution)/shard_map/cond/branch_0_fun/ppermute | solution.py:37
  52.1 14.4 %collective-permute-start.7 = (bf16[256,1024]{1,0:T(8,128)(2,1)S(1)}, bf16[256,1024]{1,0:T(8,128)(2,1)}, u32[]{:S(2)}, u32[]{:S(2)}) collective-permute-start(bf16[256,1024]{1,0:T(8,128)(2,1)S(1)} %get-tuple-element.62.refs_4_), channel_id=1, source_target_pairs={{0,1},{1,0},{2,3},{3,2},{4,5},{5,4},{6,7},{7,6},{8,9},{9,8},{10,11... | collective-permute-start | bytes 1572872 | tf_op jit(solution)/shard_map/cond/branch_0_fun/ppermute | solution.py:37
  53.6 17.1 %collective-permute-start = (bf16[256,1024]{1,0:T(8,128)(2,1)}, bf16[256,1024]{1,0:T(8,128)(2,1)}, u32[]{:S(2)}, u32[]{:S(2)}) collective-permute-start(bf16[256,1024]{1,0:T(8,128)(2,1)} %slice.40), channel_id=1, source_target_pairs={{0,8},{24,16},{1,9},{25,17},{2,10},{26,18},{3,11},{27,19},{4,12},{... | collective-permute-start | bytes 1572872 | tf_op jit(solution)/shard_map/cond/branch_0_fun/ppermute | solution.py:37
  59.2 1.8 copy-start.15
  59.2 7.3 %copy-start.13 = (bf16[512,512]{1,0:T(8,128)(2,1)S(1)}, bf16[512,512]{1,0:T(8,128)(2,1)}, u32[]{:S(2)}) copy-start(bf16[512,512]{1,0:T(8,128)(2,1)} %get-tuple-element.60) | copy-start | bytes 1572868 | tf_op jit(solution)/shard_map/cond
  59.2 11.5 %copy-start.11 = (bf16[512,512]{1,0:T(8,128)(2,1)S(1)}, bf16[512,512]{1,0:T(8,128)(2,1)}, u32[]{:S(2)}) copy-start(bf16[512,512]{1,0:T(8,128)(2,1)} %get-tuple-element.57) | copy-start | bytes 1572868 | tf_op jit(solution)/shard_map/cond
  59.3 16.1 %collective-permute-start.6 = (bf16[256,1024]{1,0:T(8,128)(2,1)S(1)}, bf16[256,1024]{1,0:T(8,128)(2,1)S(1)}, u32[]{:S(2)}, u32[]{:S(2)}) collective-permute-start(bf16[256,1024]{1,0:T(8,128)(2,1)S(1)} %collective-permute-done.5.refs_2_), channel_id=1, source_target_pairs={{0,2},{2,0},{4,6},{6,4},{1,3},{3,1},{5,7},{7,5},{8,10},{10,8},{12,... | collective-permute-start | bytes 1572872 | tf_op jit(solution)/shard_map/cond/branch_0_fun/ppermute | solution.py:37
  61.0 21.7 %collective-permute-start.10 = (bf16[512,512]{1,0:T(8,128)(2,1)S(1)}, bf16[512,512]{1,0:T(8,128)(2,1)S(1)}, u32[]{:S(2)}, u32[]{:S(2)}) collective-permute-start(bf16[512,512]{1,0:T(8,128)(2,1)S(1)} %copy-done.15), channel_id=1, source_target_pairs={{0,8},{8,0},{16,24},{24,16},{1,9},{9,1},{17,25},{25,17},{2,10},{10... | collective-permute-start | bytes 1572872 | tf_op jit(solution)/shard_map/cond/branch_0_fun/ppermute | solution.py:37
  66.5 26.5 %collective-permute-start.3 = (bf16[512,512]{1,0:T(8,128)(2,1)S(1)}, bf16[512,512]{1,0:T(8,128)(2,1)S(1)}, u32[]{:S(2)}, u32[]{:S(2)}) collective-permute-start(bf16[512,512]{1,0:T(8,128)(2,1)S(1)} %copy-done.13), channel_id=1, source_target_pairs={{0,8},{8,0},{16,24},{24,16},{1,9},{9,1},{17,25},{25,17},{2,10},{10... | collective-permute-start | bytes 1572872 | tf_op jit(solution)/shard_map/cond/branch_0_fun/ppermute | solution.py:37
  70.7 32.9 %collective-permute-start.8 = (bf16[512,512]{1,0:T(8,128)(2,1)S(1)}, bf16[512,512]{1,0:T(8,128)(2,1)S(1)}, u32[]{:S(2)}, u32[]{:S(2)}) collective-permute-start(bf16[512,512]{1,0:T(8,128)(2,1)S(1)} %copy-done.11), channel_id=1, source_target_pairs={{0,8},{8,0},{16,24},{24,16},{1,9},{9,1},{17,25},{25,17},{2,10},{10... | collective-permute-start | bytes 1572872 | tf_op jit(solution)/shard_map/cond/branch_0_fun/ppermute | solution.py:37
  73.2 31.8 %collective-permute-start.17 = (bf16[320,1024]{1,0:T(8,128)(2,1)S(1)}, bf16[320,1024]{1,0:T(8,128)(2,1)S(1)}, u32[]{:S(2)}, u32[]{:S(2)}) collective-permute-start(bf16[320,1024]{1,0:T(8,128)(2,1)S(1)} %add_convert_fusion.1), channel_id=1, source_target_pairs={{8,16},{16,8},{9,17},{17,9},{10,18},{18,10},{11,19},{19,11},{12,20... | collective-permute-start | bytes 1966088 | tf_op jit(solution)/shard_map/cond/branch_0_fun/ppermute | solution.py:37
  75.4 35.1 %collective-permute-start.20 = (bf16[320,1024]{1,0:T(8,128)(2,1)S(1)}, bf16[320,1024]{1,0:T(8,128)(2,1)S(1)}, u32[]{:S(2)}, u32[]{:S(2)}) collective-permute-start(bf16[320,1024]{1,0:T(8,128)(2,1)S(1)} %add_convert_fusion), channel_id=1, source_target_pairs={{8,16},{16,8},{9,17},{17,9},{10,18},{18,10},{11,19},{19,11},{12,20... | collective-permute-start | bytes 1966088 | tf_op jit(solution)/shard_map/cond/branch_0_fun/ppermute | solution.py:37
  77.1 4.8 %copy-start.2 = (bf16[1024,1024]{1,0:T(8,128)(2,1)S(1)}, bf16[1024,1024]{1,0:T(8,128)(2,1)}, u32[]{:S(2)}) copy-start(bf16[1024,1024]{1,0:T(8,128)(2,1)} %get-tuple-element.26.older_ref) | copy-start | bytes 6291460 | tf_op jit(solution)/shard_map/cond
  78.7 3.2 %copy-start = (bf16[1024,1024]{1,0:T(8,128)(2,1)S(1)}, bf16[1024,1024]{1,0:T(8,128)(2,1)}, u32[]{:S(2)}) copy-start(bf16[1024,1024]{1,0:T(8,128)(2,1)} %get-tuple-element.25.own_ref) | copy-start | bytes 6291460 | tf_op jit(solution)/shard_map/cond
  82.7 28.1 %collective-permute-start.13 = (bf16[256,1024]{1,0:T(8,128)(2,1)S(1)}, bf16[256,1024]{1,0:T(8,128)(2,1)S(1)}, u32[]{:S(2)}, u32[]{:S(2)}) collective-permute-start(bf16[256,1024]{1,0:T(8,128)(2,1)S(1)} %get-tuple-element.61.refs_4_), channel_id=1, source_target_pairs={{0,1},{1,0},{2,3},{3,2},{4,5},{5,4},{6,7},{7,6},{8,9},{9,8},{10,11... | collective-permute-start | bytes 1572872 | tf_op jit(solution)/shard_map/cond/branch_0_fun/ppermute | solution.py:37
  93.0 20.8 %collective-permute-start.23 = (bf16[128,1024]{1,0:T(8,128)(2,1)S(1)}, bf16[128,1024]{1,0:T(8,128)(2,1)S(1)}, u32[]{:S(2)}, u32[]{:S(2)}) collective-permute-start(bf16[128,1024]{1,0:T(8,128)(2,1)S(1)} %add_convert_fusion.3), channel_id=1, source_target_pairs={{8,16},{16,8},{9,17},{17,9},{10,18},{18,10},{11,19},{19,11},{12,20... | collective-permute-start | bytes 786440 | tf_op jit(solution)/shard_map/cond/branch_0_fun/ppermute | solution.py:37
  103.5 10.4 %collective-permute-start.1 = (bf16[256,1024]{1,0:T(8,128)(2,1)S(1)}, bf16[256,1024]{1,0:T(8,128)(2,1)S(1)}, u32[]{:S(2)}, u32[]{:S(2)}) collective-permute-start(bf16[256,1024]{1,0:T(8,128)(2,1)S(1)} %add_convert_fusion.2), channel_id=1, source_target_pairs={{8,16},{16,8},{9,17},{17,9},{10,18},{18,10},{11,19},{19,11},{12,20... | collective-permute-start | bytes 1572872 | tf_op jit(solution)/shard_map/cond/branch_0_fun/ppermute | solution.py:37
  105.0 73.4 %collective-permute-start.14 = (bf16[512,512]{1,0:T(8,128)(2,1)S(1)}, bf16[512,512]{1,0:T(8,128)(2,1)S(1)}, u32[]{:S(2)}, u32[]{:S(2)}) collective-permute-start(bf16[512,512]{1,0:T(8,128)(2,1)S(1)} %branch_0_fun.16.refs_2_.refs_0_), channel_id=1, source_target_pairs={{0,16},{8,24},{16,0},{24,8},{1,17},{9,25},{17,1},{25,9},{2,18},{10... | collective-permute-start | bytes 1572872 | tf_op jit(solution)/shard_map/cond/branch_0_fun/ppermute | solution.py:37
  110.5 79.2 %collective-permute-start.11 = (bf16[512,512]{1,0:T(8,128)(2,1)S(1)}, bf16[512,512]{1,0:T(8,128)(2,1)S(1)}, u32[]{:S(2)}, u32[]{:S(2)}) collective-permute-start(bf16[512,512]{1,0:T(8,128)(2,1)S(1)} %branch_0_fun.14.refs_0_), channel_id=1, source_target_pairs={{0,16},{8,24},{16,0},{24,8},{1,17},{9,25},{17,1},{25,9},{2,18},{10... | collective-permute-start | bytes 1572872 | tf_op jit(solution)/shard_map/cond/branch_0_fun/ppermute | solution.py:37
  110.8 124.2 %collective-permute-start.15 = (bf16[512,512]{1,0:T(8,128)(2,1)S(1)}, bf16[512,512]{1,0:T(8,128)(2,1)S(1)}, u32[]{:S(2)}, u32[]{:S(2)}) collective-permute-start(bf16[512,512]{1,0:T(8,128)(2,1)S(1)} %branch_0_fun.17.refs_3_.refs_1_), channel_id=1, source_target_pairs={{0,16},{8,24},{16,0},{24,8},{1,17},{9,25},{17,1},{25,9},{2,18},{10... | collective-permute-start | bytes 1572872 | tf_op jit(solution)/shard_map/cond/branch_0_fun/ppermute | solution.py:37
  113.8 96.8 %collective-permute-start.12 = (bf16[512,512]{1,0:T(8,128)(2,1)S(1)}, bf16[512,512]{1,0:T(8,128)(2,1)S(1)}, u32[]{:S(2)}, u32[]{:S(2)}) collective-permute-start(bf16[512,512]{1,0:T(8,128)(2,1)S(1)} %branch_0_fun.15.refs_1_), channel_id=1, source_target_pairs={{0,16},{8,24},{16,0},{24,8},{1,17},{9,25},{17,1},{25,9},{2,18},{10... | collective-permute-start | bytes 1572872 | tf_op jit(solution)/shard_map/cond/branch_0_fun/ppermute | solution.py:37
  113.9 144.6 %collective-permute-start.18 = (bf16[320,1024]{1,0:T(8,128)(2,1)S(1)}, bf16[320,1024]{1,0:T(8,128)(2,1)S(1)}, u32[]{:S(2)}, u32[]{:S(2)}) collective-permute-start(bf16[320,1024]{1,0:T(8,128)(2,1)S(1)} %multiply_convert_fusion.1.refs_0_), channel_id=1, source_target_pairs={{8,0},{16,24},{9,1},{17,25},{10,2},{18,26},{11,3},{19,27},{12,4},{... | collective-permute-start | bytes 1966088 | tf_op jit(solution)/shard_map/cond/branch_0_fun/ppermute | solution.py:37
  178.4 77.9 %collective-permute-start.21 = (bf16[320,1024]{1,0:T(8,128)(2,1)S(1)}, bf16[320,1024]{1,0:T(8,128)(2,1)S(1)}, u32[]{:S(2)}, u32[]{:S(2)}) collective-permute-start(bf16[320,1024]{1,0:T(8,128)(2,1)S(1)} %multiply_convert_fusion.refs_0_), channel_id=1, source_target_pairs={{8,0},{16,24},{9,1},{17,25},{10,2},{18,26},{11,3},{19,27},{12,4},{... | collective-permute-start | bytes 1966088 | tf_op jit(solution)/shard_map/cond/branch_0_fun/ppermute | solution.py:37
  189.7 71.1 %collective-permute-start.2 = (bf16[256,1024]{1,0:T(8,128)(2,1)S(1)}, bf16[256,1024]{1,0:T(8,128)(2,1)S(1)}, u32[]{:S(2)}, u32[]{:S(2)}) collective-permute-start(bf16[256,1024]{1,0:T(8,128)(2,1)S(1)} %multiply_convert_fusion.2.refs_0_), channel_id=1, source_target_pairs={{8,0},{16,24},{9,1},{17,25},{10,2},{18,26},{11,3},{19,27},{12,4},{... | collective-permute-start | bytes 1572872 | tf_op jit(solution)/shard_map/cond/branch_0_fun/ppermute | solution.py:37
  210.7 44.8 %collective-permute-start.24 = (bf16[128,1024]{1,0:T(8,128)(2,1)S(1)}, bf16[128,1024]{1,0:T(8,128)(2,1)S(1)}, u32[]{:S(2)}, u32[]{:S(2)}) collective-permute-start(bf16[128,1024]{1,0:T(8,128)(2,1)S(1)} %multiply_convert_fusion.3.refs_0_), channel_id=1, source_target_pairs={{8,0},{16,24},{9,1},{17,25},{10,2},{18,26},{11,3},{19,27},{12,4},{... | collective-permute-start | bytes 786440 | tf_op jit(solution)/shard_map/cond/branch_0_fun/ppermute | solution.py:37
  261.8 1.3 copy-start.8

commit v2 on v1

--- a/solution.py
+++ b/solution.py
@@ -15,8 +15,8 @@
 NS_ITERS = 2
 STEPS = 2
 SPLIT = 2
-NEAR_SHARES = (2, 5, 5, 4)
-FAR_SHARES = (5, 5, 4, 2)
+NEAR_PLAN = ((4, 4, 4, 4), 3, False)
+FAR_PLAN = ((4, 4, 4, 4), 2, True)
 TILE = 256
 
 quintic_a = 3.4445
@@ -35,6 +35,16 @@
 
 def send(x, axis, route):
     return lax.ppermute(x, axis, route)
+
+
+def swap(x, mask, relay):
+    count = lax.axis_size("rep")
+    if not relay or count != 4 or mask != 2:
+        return [send(x, "rep", xor_route(count, mask))]
+    inward = send(x, "rep", [(0, 1), (3, 2)])
+    to_inner = send(inward, "rep", [(1, 2), (2, 1)])
+    across = send(x, "rep", [(1, 2), (2, 1)])
+    return [to_inner, send(across, "rep", [(1, 0), (2, 3)])]
 
 
 def gather_pieces(x, axis):
@@ -69,7 +79,15 @@
     x_ref[...] = (quintic_a * x.astype(f32) + dot(x, poly)).astype(bf16)
 
 
-def call(kernel, out_shape, mib=16, **kw):
+def in_hbm(x):
+    return pltpu.with_memory_space_constraint(x, pltpu.HBM)
+
+
+def single(shape, index):
+    return pl.BlockSpec(shape, index, pipeline_mode=pl.Buffered(1))
+
+
+def call(kernel, out_shape, mib=12, **kw):
     params = pltpu.CompilerParams(vmem_limit_bytes=mib << 20)
     return pl.pallas_call(kernel, out_shape=out_shape, compiler_params=params, **kw)
 
@@ -105,7 +123,7 @@
         for g in range(count_g):
             turned_ref[:, g * tokens : (g + 1) * tokens] = grads[g][...].T
 
-    whole = lambda *shape: pl.BlockSpec(shape, lambda i: (0,) * len(shape))
+    whole = lambda *shape: single(shape, lambda i: (0,) * len(shape))
     return call(
         kernel,
         (jax.ShapeDtypeStruct((total, cols), bf16), jax.ShapeDtypeStruct((rows, total), bf16)),
@@ -117,32 +135,34 @@
     )(pool_bases, token_ids, *pool_pieces, *grad_pieces)
 
 
-def first_mix(own, other, older, turned, chosen, row, col, height, width):
-    def kernel(own_ref, other_ref, older_ref, turned_ref, chosen_ref, out_ref):
+def first_mix(own, others, older, turned, chosen, row, col, height, width):
+    def kernel(own_ref, older_ref, turned_ref, chosen_ref, *refs):
+        *other_refs, out_ref = refs
+
         def mix(k):
             t = tile(k, TILE)
             fresh = dot(turned_ref[t, :], chosen_ref[...])
-            mean = 0.5 * (own_ref[t, :].astype(f32) + other_ref[t, :].astype(f32))
+            mean = 0.5 * (own_ref[t, :].astype(f32) + sum(r[t, :].astype(f32) for r in other_refs))
             out_ref[t, :] = (mean + fresh - older_ref[t, :].astype(f32)).astype(bf16)
 
         loop(height // TILE, mix)
 
     tokens = chosen.shape[0]
-    piece = pl.BlockSpec((height, width), lambda i: (row, col))
-    alone = pl.BlockSpec((height, width), lambda i: (0, 0))
+    piece = single((height, width), lambda i: (row, col))
+    alone = single((height, width), lambda i: (0, 0))
     return call(
         kernel,
         jax.ShapeDtypeStruct((height, width), bf16),
         grid=(1,),
         in_specs=[
             piece,
-            alone,
             piece,
-            pl.BlockSpec((height, tokens), lambda i: (row, 0)),
-            pl.BlockSpec((tokens, width), lambda i: (0, col)),
-        ],
+            single((height, tokens), lambda i: (row, 0)),
+            single((tokens, width), lambda i: (0, col)),
+        ]
+        + [alone] * len(others),
         out_specs=alone,
-    )(own, other, older, turned, chosen)
+    )(in_hbm(own), in_hbm(older), turned, chosen, *others)
 
 
 def stacked(refs):
@@ -165,105 +185,135 @@
     loop(count, scale)
 
 
-def orthogonal(blocks):
-    pieces = len(blocks[0])
-    height, width = blocks[0][0].shape
-    height *= pieces
+def orthogonal(pieces):
+    height, width = pieces[0].shape
+    height *= len(pieces)
 
     def kernel(*refs):
-        x_ref = refs[-1]
-        for k in range(len(blocks)):
-            x_ref[k] = stacked(refs[k * pieces : (k + 1) * pieces])
-        newton_schulz(x_ref, len(blocks))
-
-    return call(
-        kernel, jax.ShapeDtypeStruct((len(blocks), height, width), bf16)
-    )(*[piece for block in blocks for piece in block])
-
-
-def second_mix(mine, theirs, grads, row, col, whole, previous):
+        refs[-1][0] = stacked(refs[:-1])
+        newton_schulz(refs[-1], 1)
+
+    return call(kernel, jax.ShapeDtypeStruct((1, height, width), bf16))(*pieces)
+
+
+def sliver(*sizes):
+    return math.gcd(64, *sizes)
+
+
+def second_mix(mine, theirs, grads, first, means, scale, block, whole, previous):
     pieces = len(mine)
     height, width = mine[0].shape
     height *= pieces
+    sizes = [parts[0].shape[0] for parts in means]
+    early = sum(sizes)
+    flat = [part for parts in means for part in parts]
+    each = len(flat) // len(means)
+    received, parts = [part for pieces_of in theirs for part in pieces_of], len(theirs[0])
+    cut = slice(block * width, (block + 1) * width)
+    outs = 3 if early < height else 2
 
     def kernel(*refs):
-        mine_refs, theirs_refs = refs[:pieces], refs[pieces : 2 * pieces]
-        turned_1, chosen_1, turned_0, chosen_0 = refs[2 * pieces : 2 * pieces + 4]
-        tracker_ref, update_ref, x_ref, y_ref = refs[-4:]
-        x_ref[0] = stacked(theirs_refs)
+        mine_refs, refs = refs[:pieces], refs[pieces:]
+        theirs_refs, refs = refs[: len(received)], refs[len(received) :]
+        turned_1, chosen_1, turned_0, chosen_0, first_ref = refs[:5]
+        mean_refs = refs[5 : 5 + len(flat)]
+        *out_refs, x_ref, y_ref, tracker_ref, weights_ref, sems = refs[-outs - 5 :]
+        x_ref[0] = sum(stacked(theirs_refs[part::parts]) for part in range(parts))
         y_ref[...] = stacked(mine_refs)
 
         def mix(k):
             t = tile(k, TILE)
-            fresh = dot(turned_1[t, :], chosen_1[...]) - dot(turned_0[t, :], chosen_0[...])
+            fresh = dot(turned_1[t, :], chosen_1[:, cut]) - dot(turned_0[t, :], chosen_0[:, cut])
             mean = 0.5 * (y_ref[t, :].astype(f32) + x_ref[0, t, :].astype(f32))
             mixed = (mean + fresh).astype(bf16)
             tracker_ref[t, :] = mixed
             x_ref[1, t, :] = mixed
 
+        def update(t):
+            both = first_ref[0, t, :].astype(f32) + x_ref[0, t, :].astype(f32)
+            return 0.5 * both + x_ref[1, t, :].astype(f32)
+
         loop(height // TILE, mix)
+        tracker_copy = pltpu.make_async_copy(tracker_ref, out_refs[0].at[0, :, cut], sems.at[0])
+        tracker_copy.start()
         newton_schulz(x_ref, 2)
-        update_ref[...] = 0.5 * x_ref[0].astype(f32) + x_ref[1].astype(f32)
-
-    alone = pl.BlockSpec((height // pieces, width), lambda i: (0, 0))
-    operands = [*mine, *theirs, *grads]
-    in_specs = [alone] * (2 * pieces)
-    for turned, chosen in zip(grads[::2], grads[1::2]):
-        in_specs += [pl.BlockSpec((height, turned.shape[1]), lambda i: (row, 0))]
-        in_specs += [pl.BlockSpec((chosen.shape[0], width), lambda i: (0, col))]
+        at = 0
+        for p, size in enumerate(sizes):
+            unit = sliver(size, at)
+
+            def weigh(k, at=at, unit=unit, parts=mean_refs[p * each : (p + 1) * each]):
+                mean = sum(r[tile(k, unit), cut].astype(f32) for r in parts)
+                t = pl.ds(pl.multiple_of(at + k * unit, unit), unit)
+                weights_ref[t, :] = (mean - scale * update(t)).astype(bf16)
+
+            loop(size // unit, weigh)
+            at += size
+        weights_copy = pltpu.make_async_copy(weights_ref, out_refs[1].at[0, :early, cut], sems.at[1])
+        weights_copy.start()
+        if outs == 3:
+            unit = sliver(height - early, early)
+
+            def keep(k):
+                t = pl.ds(pl.multiple_of(early + k * unit, unit), unit)
+                out_refs[2][tile(k, unit), :] = update(t)
+
+            loop((height - early) // unit, keep)
+        tracker_copy.wait()
+        weights_copy.wait()
+
+    vmem = pl.BlockSpec(memory_space=pltpu.VMEM)
+    apart = pl.BlockSpec(memory_space=pltpu.HBM)
+    operands = [*mine, *received, *grads, first, *flat]
+    in_specs = [vmem] * len(operands)
     aliases = {}
     if previous is not None:
-        aliases = {len(operands): 0}
-        operands += [previous]
-        in_specs += [pl.BlockSpec(memory_space=pl.ANY)]
+        aliases = {len(operands): 0, len(operands) + 1: 1}
+        operands += list(previous)
+        in_specs += [apart] * 2
+    out_shape = [jax.ShapeDtypeStruct((1, *whole), bf16)] * 2
+    if outs == 3:
+        out_shape += [jax.ShapeDtypeStruct((height - early, width), f32)]
     return call(
         kernel,
-        mib=32,
-        out_shape=(jax.ShapeDtypeStruct((1, *whole), bf16), jax.ShapeDtypeStruct((height, width), f32)),
-        grid=(1,),
+        mib=24,
+        out_shape=out_shape,
         in_specs=in_specs,
-        out_specs=(
-            pl.BlockSpec((None, height, width), lambda i: (0, row, col)),
-            pl.BlockSpec((height, width), lambda i: (0, 0)),
-        ),
-        scratch_shapes=[pltpu.VMEM((2, height, width), bf16), pltpu.VMEM((height, width), bf16)],
+        out_specs=[apart] * 2 + [vmem] * (outs - 2),
+        scratch_shapes=[
+            pltpu.VMEM((2, height, width), bf16),
+            pltpu.VMEM((height, width), bf16),
+            pltpu.VMEM((height, width), bf16),
+            pltpu.VMEM((early, width), bf16),
+            pltpu.SemaphoreType.DMA((2,)),
+        ],
         input_output_aliases=aliases,
     )(*operands)
 
 
-def apply(means, first, updates, scale, at, blocks, whole, previous):
+def apply(means, updates, scale, at, start, whole, previous):
     rows, cols = means[0].shape
-    _, height, width = first.shape
-    unit = math.gcd(at, rows) if at else rows
-    steps = rows // unit
+    unit = math.gcd(rows, at, at - start) if at > start else math.gcd(rows, at)
+    width = updates[0].shape[1]
 
     def kernel(*refs):
-        mean_refs, (first_ref, *update_refs) = refs[: len(means)], refs[len(means) : len(operands)]
+        mean_refs, update_refs = refs[: len(means)], refs[len(means) : len(means) + len(updates)]
         out_ref = refs[-1]
-        for c in range(blocks):
+        for c, update_ref in enumerate(update_refs):
             cut = slice(c * width, (c + 1) * width)
             mean = sum(r[:, cut].astype(f32) for r in mean_refs)
-            update = 0.5 * first_ref[c].astype(f32) + update_refs[c][...]
-            out_ref[:, cut] = (mean - scale * update).astype(bf16)
-
-    row = at // height
-    into = lambda i: (at % height) // unit + i
-    operands = [*means, first, *updates[row * blocks : (row + 1) * blocks]]
-    in_specs = [pl.BlockSpec((unit, cols), lambda i: (i, 0))] * len(means)
-    in_specs += [pl.BlockSpec((blocks, unit, width), lambda i: (row, into(i), 0))]
-    in_specs += [pl.BlockSpec((unit, width), lambda i: (into(i), 0))] * blocks
-    aliases = {}
-    if previous is not None:
-        aliases = {len(operands): 0}
-    call_operands = operands + ([previous] if previous is not None else [])
+            out_ref[:, cut] = (mean - scale * update_ref[...]).astype(bf16)
+
+    operands = [*means, *updates, previous]
     return call(
         kernel,
         jax.ShapeDtypeStruct((1, *whole), bf16),
-        grid=(steps,),
-        in_specs=in_specs + [pl.BlockSpec(memory_space=pl.ANY)] * len(aliases),
+        grid=(rows // unit,),
+        in_specs=[pl.BlockSpec((unit, cols), lambda i: (i, 0))] * len(means)
+        + [pl.BlockSpec((unit, width), lambda i: ((at - start) // unit + i, 0))] * len(updates)
+        + [pl.BlockSpec(memory_space=pl.ANY)],
         out_specs=pl.BlockSpec((None, unit, cols), lambda i: (0, at // unit + i, 0)),
-        input_output_aliases=aliases,
-    )(*call_operands)
+        input_output_aliases={len(operands) - 1: 0},
+    )(*operands)
 
 
 def mean_of_four(own, first_route, second_route):
@@ -288,6 +338,7 @@
     count = lax.axis_size("rep")
     rows, cols = weights.shape
     height, width = QOUT // GRID, D // GRID
+    assert rows == height and cols % width == 0
     piece = height // SPLIT
     scale = 0.2 * math.sqrt(QOUT // GRID)
     first_route, second_route = xor_route(count, first_mask), xor_route(count, second_mask)
@@ -313,35 +364,38 @@
     def part(x, r, c):
         return lax.slice(x, (r * piece, c * width), ((r + 1) * piece, (c + 1) * width))
 
-    blocks = [(r, c) for r in range(rows // height) for c in range(cols // width)]
+    shares, early, relay = NEAR_PLAN if first_mask == 1 else FAR_PLAN
     mine, theirs = [], []
-    for row, col in blocks:
+    for col in range(cols // width):
         mine.append([])
         theirs.append([])
-        for s in range(SPLIT):
-            r = row * SPLIT + s
-            other = send(part(tracker, r, col), "rep", first_route)
-            mixed = first_mix(tracker, other, grad_prev, *grads[2:], r, col, piece, width)
+        for r in range(SPLIT):
+            k = col * SPLIT + r
+            others = swap(part(tracker, r, col), first_mask, relay)
+            mixed = first_mix(tracker, others, grad_prev, *grads[2:], r, col, piece, width)
             mine[-1].append(mixed)
-            theirs[-1].append(send(mixed, "rep", second_route))
-    first = orthogonal(mine)
-    new_tracker, updates = None, []
-    for b, (row, col) in enumerate(blocks):
-        new_tracker, update = second_mix(
-            mine[b], theirs[b], grads, row, col, weights.shape, new_tracker
-        )
+            theirs[-1].append(swap(mixed, second_mask, relay))
+    first = [orthogonal(mine[col]) for col in range(len(mine))]
+
+    ends = [rows * sum(shares[: k + 1]) // sum(shares) for k in range(len(shares))]
+    cuts = list(zip([0, *ends], ends))
+    means = []
+    for k, (low, high) in enumerate(cuts):
+        own = lax.optimization_barrier(lax.slice_in_dim(weights, low, high))
+        means.append(mean_of_four(own, first_route, second_route))
+
+    results, updates = None, []
+    for col in range(cols // width):
+        *results, update = *second_mix(
+            mine[col], theirs[col], grads, first[col], means[:early], scale, col,
+            weights.shape, results,
+        ), None
+        if early < len(shares):
+            *results, update = results
         updates.append(update)
-
-    new_weights, at = None, 0
-    shares = NEAR_SHARES if first_mask == 1 else FAR_SHARES
-    for share in shares:
-        size = rows * share // sum(shares)
-        own = lax.optimization_barrier(lax.slice_in_dim(weights, at, at + size))
-        means = mean_of_four(own, first_route, second_route)
-        new_weights = apply(
-            means, first, updates, scale, at, cols // width, weights.shape, new_weights
-        )
-        at += size
+    new_tracker, new_weights = results
+    for k in range(early, len(shares)):
+        new_weights = apply(means[k], updates, scale, cuts[k][0], cuts[early][0], weights.shape, new_weights)
     return new_weights, new_tracker
 
 

time: 264 us -> 228 us (0.86)
  the two profiles are of different devices: /device:TPU:0 before, /device:TPU:8 now
where the time goes in v2:
time: 228 us; the launch traced here: 227 us
  waiting for transfers between devices  132 us (58%)
  Pallas kernels  46.5 us (20%)
  starting transfers between devices  38 us (17%)
  local copies, waits for them, and re-layouts  4.7 us (2%)
  other arithmetic  4.03 us (2%)
    ppermute x25, waiting for transfers between devices, send(): return lax.ppermute(x, axis, route)  132 us
    ppermute x25, starting transfers between devices, send(): return lax.ppermute(x, axis, route)  38 us
    pallas_call x2, Pallas kernels, second_mix(): call(kernel, mib=24, out_shape=out_shape, in_specs=in_specs, out_specs=[a...  24.6 us
    pallas_call x2, Pallas kernels, orthogonal(): return call(kernel, jax.ShapeDtypeStruct((1, height, width), bf16))(*pieces)  8.73 us
    pallas_call x4, Pallas kernels, first_mix(): call(kernel, jax.ShapeDtypeStruct((height, width), bf16), grid=(1,), in_s...  7.45 us
    pallas_call x2, Pallas kernels, prepare(): call(kernel, (jax.ShapeDtypeStruct((total, cols), bf16), jax.ShapeDtypeSt...  4.74 us
  transfers between devices with their start and end apart: 25, of which 12 were waited for; matrix products, arithmetic and copies ran while one was open for 4% of the time, Pallas kernels for 20%

profile of v2, /device:TPU:8, one launch (start us, length us, event | category | flops | bytes accessed | tf_op | source)
XLA Modules:
  0.0 227.1 jit_solution(2853433583113149196)
XLA Ops:
  1.3 225.8 %conditional.1 = (bf16[1,1024,1024]{2,1,0:T(8,128)(2,1)}, bf16[1,1024,1024]{2,1,0:T(8,128)(2,1)}) conditional(s32[]{:T(128)} %clamp.3, (bf16[1024,1024]{1,0:T(8,128)(2,1)}, s32[2,512]{1,0:T(2,128)}, bf16[256,1024]{1,0:T(8,128)(2,1)}, bf16[2,256,1024]{2,1,0:T(8,128)(2,1)}, bf16[1024,1024]{1,0:T(8,128)(2,1)}, ...), branch_computations={%region_0.1_spmd, %region_1.2_spmd} | conditional | flops 9440296 | bytes 144746704 | solution.py:408
  1.3 0.0 copy-start.3
  1.3 1.6 collective-permute-start.4
  2.9 1.3 slice_bitcast_fusion
  4.2 1.6 collective-permute-start.6
  5.7 1.3 fusion
  7.1 1.3 collective-permute-start.12
  8.4 1.3 collective-permute-start.15
  9.7 0.1 constant_dynamic-slice_fusion.1
  9.8 0.2 copy.18.ids_ref
  10.0 0.1 add_multiply_fusion.base_ref
  10.1 1.8 fusion.1
  11.9 3.4 %collective-permute-done.4.refs_2_ = bf16[256,1024]{1,0:T(8,128)(2,1)S(1)} collective-permute-done((bf16[256,1024]{1,0:T(8,128)(2,1)}, bf16[256,1024]{1,0:T(8,128)(2,1)S(1)}, u32[]{:S(2)}, u32[]{:S(2)}) %collective-permute-start.4) | collective-permute-done | bytes 524320 | tf_op jit(solution)/shard_map/cond/branch_0_fun/ppermute | solution.py:37
  15.3 0.9 collective-permute-start.7
  16.2 0.0 collective-permute-done.3.refs_1_
  16.2 1.3 collective-permute-start.18
  17.4 6.6 %collective-permute-done.12 = bf16[256,1024]{1,0:T(8,128)(2,1)} collective-permute-done((bf16[256,1024]{1,0:T(8,128)(2,1)}, bf16[256,1024]{1,0:T(8,128)(2,1)}, u32[]{:S(2)}, u32[]{:S(2)}) %collective-permute-start.12) | collective-permute-done | bytes 524320 | tf_op jit(solution)/shard_map/cond/branch_0_fun/ppermute | solution.py:37
  24.1 1.3 collective-permute-start
  25.4 1.4 add_convert_fusion.2
  26.8 0.0 copy-start.5
  26.8 8.5 %collective-permute-done.15 = bf16[256,1024]{1,0:T(8,128)(2,1)} collective-permute-done((bf16[256,1024]{1,0:T(8,128)(2,1)}, bf16[256,1024]{1,0:T(8,128)(2,1)}, u32[]{:S(2)}, u32[]{:S(2)}) %collective-permute-start.15) | collective-permute-done | bytes 524320 | tf_op jit(solution)/shard_map/cond/branch_0_fun/ppermute | solution.py:37
  35.3 1.4 add_convert_fusion.1
  36.7 0.1 collective-permute-start.8
  36.8 9.6 %collective-permute-done.7.refs_0_ = bf16[512,512]{1,0:T(8,128)(2,1)S(1)} collective-permute-done((bf16[512,512]{1,0:T(8,128)(2,1)S(1)}, bf16[512,512]{1,0:T(8,128)(2,1)S(1)}, u32[]{:S(2)}, u32[]{:S(2)}) %collective-permute-start.7) | collective-permute-done | bytes 524320 | tf_op jit(solution)/shard_map/cond/branch_0_fun/ppermute | solution.py:37
  46.4 11.2 %collective-permute-done.18 = bf16[256,1024]{1,0:T(8,128)(2,1)S(1)} collective-permute-done((bf16[256,1024]{1,0:T(8,128)(2,1)S(1)}, bf16[256,1024]{1,0:T(8,128)(2,1)S(1)}, u32[]{:S(2)}, u32[]{:S(2)}) %collective-permute-start.18) | collective-permute-done | bytes 524320 | tf_op jit(solution)/shard_map/cond/branch_0_fun/ppermute | solution.py:37
  57.7 0.0 collective-permute-start.21
  57.7 11.2 %collective-permute-done = bf16[256,1024]{1,0:T(8,128)(2,1)S(1)} collective-permute-done((bf16[256,1024]{1,0:T(8,128)(2,1)S(1)}, bf16[256,1024]{1,0:T(8,128)(2,1)S(1)}, u32[]{:S(2)}, u32[]{:S(2)}) %collective-permute-start) | collective-permute-done | bytes 524320 | tf_op jit(solution)/shard_map/cond/branch_0_fun/ppermute | solution.py:37
  68.9 3.5 %collective-permute-start.13 = (bf16[256,1024]{1,0:T(8,128)(2,1)S(1)}, bf16[256,1024]{1,0:T(8,128)(2,1)S(1)}, u32[]{:S(2)}, u32[]{:S(2)}) collective-permute-start(bf16[256,1024]{1,0:T(8,128)(2,1)S(1)} %add_convert_fusion.2), channel_id=1, source_target_pairs={{8,16},{16,8},{9,17},{17,9},{10,18},{18,10},{11,19},{19,11},{12,20... | collective-permute-start | bytes 1572872 | tf_op jit(solution)/shard_map/cond/branch_0_fun/ppermute | solution.py:37
  72.4 0.2 add_convert_fusion
  72.6 2.4 %collective-permute-start.16 = (bf16[256,1024]{1,0:T(8,128)(2,1)S(1)}, bf16[256,1024]{1,0:T(8,128)(2,1)S(1)}, u32[]{:S(2)}, u32[]{:S(2)}) collective-permute-start(bf16[256,1024]{1,0:T(8,128)(2,1)S(1)} %add_convert_fusion.1), channel_id=1, source_target_pairs={{8,16},{16,8},{9,17},{17,9},{10,18},{18,10},{11,19},{19,11},{12,20... | collective-permute-start | bytes 1572872 | tf_op jit(solution)/shard_map/cond/branch_0_fun/ppermute | solution.py:37
  75.0 0.2 add_convert_fusion.3
  75.2 2.4 %branch_0_fun.11 = (bf16[512,1024]{1,0:T(8,128)(2,1)S(1)}, bf16[1024,512]{1,0:T(8,128)(2,1)S(1)}) custom-call(s32[4]{0:T(128)S(1)} %add_multiply_fusion.base_ref, s32[1024,1]{1,0:T(8,128)S(1)} %copy.18.ids_ref, bf16[256,1024]{1,0:T(8,128)(2,1)S(1)} %copy-done.5, bf16[256,1024]{1,0:T(8,128)(2,1)S(1)} %collective-permute-done.3.refs_1_, ...), custom_call_target="tpu_custom_call" | custom-call | tf_op jit(solution)/shard_map/cond/branch_0_fun/pallas_call | solution.py:127
  77.6 1.9 branch_0_fun.12.refs_0_
  79.4 0.7 collective-permute-done.8.refs_0_
  80.1 0.5 collective-permute-start.11
  80.7 1.9 branch_0_fun.13.refs_1_
  82.5 8.8 %collective-permute-done.22.refs_0_ = bf16[512,512]{1,0:T(8,128)(2,1)S(1)} collective-permute-done((bf16[512,512]{1,0:T(8,128)(2,1)S(1)}, bf16[512,512]{1,0:T(8,128)(2,1)S(1)}, u32[]{:S(2)}, u32[]{:S(2)}) %collective-permute-start.22) | collective-permute-done | bytes 524320 | tf_op jit(solution)/shard_map/cond/branch_0_fun/ppermute | solution.py:37
  91.4 3.5 %collective-permute-start.19 = (bf16[256,1024]{1,0:T(8,128)(2,1)S(1)}, bf16[256,1024]{1,0:T(8,128)(2,1)S(1)}, u32[]{:S(2)}, u32[]{:S(2)}) collective-permute-start(bf16[256,1024]{1,0:T(8,128)(2,1)S(1)} %add_convert_fusion), channel_id=1, source_target_pairs={{8,16},{16,8},{9,17},{17,9},{10,18},{18,10},{11,19},{19,11},{12,20... | collective-permute-start | bytes 1572872 | tf_op jit(solution)/shard_map/cond/branch_0_fun/ppermute | solution.py:37
  94.9 1.9 branch_0_fun.18.refs_1_
  96.7 5.1 %collective-permute-done.21.refs_0_ = bf16[512,512]{1,0:T(8,128)(2,1)S(1)} collective-permute-done((bf16[512,512]{1,0:T(8,128)(2,1)S(1)}, bf16[512,512]{1,0:T(8,128)(2,1)S(1)}, u32[]{:S(2)}, u32[]{:S(2)}) %collective-permute-start.21) | collective-permute-done | bytes 524320 | tf_op jit(solution)/shard_map/cond/branch_0_fun/ppermute | solution.py:37
  101.9 3.5 %collective-permute-start.1 = (bf16[256,1024]{1,0:T(8,128)(2,1)S(1)}, bf16[256,1024]{1,0:T(8,128)(2,1)S(1)}, u32[]{:S(2)}, u32[]{:S(2)}) collective-permute-start(bf16[256,1024]{1,0:T(8,128)(2,1)S(1)} %add_convert_fusion.3), channel_id=1, source_target_pairs={{8,16},{16,8},{9,17},{17,9},{10,18},{18,10},{11,19},{19,11},{12,20... | collective-permute-start | bytes 1572872 | tf_op jit(solution)/shard_map/cond/branch_0_fun/ppermute | solution.py:37
  105.4 1.9 branch_0_fun.17.refs_0_
  107.2 0.1 collective-permute-start.10
  107.3 0.2 multiply_convert_fusion.2.refs_9_
  107.5 0.0 collective-permute-done.16
  107.5 3.0 %collective-permute-start.9 = (bf16[512,512]{1,0:T(8,128)(2,1)S(1)}, bf16[512,512]{1,0:T(8,128)(2,1)S(1)}, u32[]{:S(2)}, u32[]{:S(2)}) collective-permute-start(bf16[512,512]{1,0:T(8,128)(2,1)S(1)} %branch_0_fun.12.refs_0_), channel_id=1, source_target_pairs={{0,16},{8,24},{16,0},{24,8},{1,17},{9,25},{17,1},{25,9},{2,18},{10... | collective-permute-start | bytes 1572872 | tf_op jit(solution)/shard_map/cond/branch_0_fun/ppermute | solution.py:37
  110.5 0.2 multiply_convert_fusion.1.refs_11_
  110.7 1.3 collective-permute-start.14
  112.1 0.2 multiply_convert_fusion.refs_13_
  112.3 1.3 collective-permute-start.17
  113.6 27.4 %collective-permute-done.1 = bf16[256,1024]{1,0:T(8,128)(2,1)S(1)} collective-permute-done((bf16[256,1024]{1,0:T(8,128)(2,1)S(1)}, bf16[256,1024]{1,0:T(8,128)(2,1)S(1)}, u32[]{:S(2)}, u32[]{:S(2)}) %collective-permute-start.1) | collective-permute-done | bytes 524320 | tf_op jit(solution)/shard_map/cond/branch_0_fun/ppermute | solution.py:37
  141.0 1.3 collective-permute-start.20
  142.3 20.1 %collective-permute-done.10.refs_3_ = bf16[512,512]{1,0:T(8,128)(2,1)S(1)} collective-permute-done((bf16[512,512]{1,0:T(8,128)(2,1)S(1)}, bf16[512,512]{1,0:T(8,128)(2,1)S(1)}, u32[]{:S(2)}, u32[]{:S(2)}) %collective-permute-start.10) | collective-permute-done | bytes 524320 | tf_op jit(solution)/shard_map/cond/branch_0_fun/ppermute | solution.py:37
  162.5 3.5 %collective-permute-start.24 = (bf16[512,512]{1,0:T(8,128)(2,1)S(1)}, bf16[512,512]{1,0:T(8,128)(2,1)S(1)}, u32[]{:S(2)}, u32[]{:S(2)}) collective-permute-start(bf16[512,512]{1,0:T(8,128)(2,1)S(1)} %branch_0_fun.18.refs_1_), channel_id=1, source_target_pairs={{0,16},{8,24},{16,0},{24,8},{1,17},{9,25},{17,1},{25,9},{2,18},{10... | collective-permute-start | bytes 1572872 | tf_op jit(solution)/shard_map/cond/branch_0_fun/ppermute | solution.py:37
  166.0 19.1 %collective-permute-done.9.refs_2_ = bf16[512,512]{1,0:T(8,128)(2,1)S(1)} collective-permute-done((bf16[512,512]{1,0:T(8,128)(2,1)S(1)}, bf16[512,512]{1,0:T(8,128)(2,1)S(1)}, u32[]{:S(2)}, u32[]{:S(2)}) %collective-permute-start.9) | collective-permute-done | bytes 524320 | tf_op jit(solution)/shard_map/cond/branch_0_fun/ppermute | solution.py:37
  185.2 3.4 %collective-permute-start.23 = (bf16[512,512]{1,0:T(8,128)(2,1)S(1)}, bf16[512,512]{1,0:T(8,128)(2,1)S(1)}, u32[]{:S(2)}, u32[]{:S(2)}) collective-permute-start(bf16[512,512]{1,0:T(8,128)(2,1)S(1)} %branch_0_fun.17.refs_0_), channel_id=1, source_target_pairs={{0,16},{8,24},{16,0},{24,8},{1,17},{9,25},{17,1},{25,9},{2,18},{10... | collective-permute-start | bytes 1572872 | tf_op jit(solution)/shard_map/cond/branch_0_fun/ppermute | solution.py:37
  188.6 0.2 multiply_convert_fusion.3.refs_0_
  188.8 1.5 collective-permute-start.2
  190.3 4.4 %branch_0_fun.15.refs_8_ = bf16[1,1024,512]{2,1,0:T(8,128)(2,1)S(1)} custom-call(bf16[512,512]{1,0:T(8,128)(2,1)S(1)} %branch_0_fun.12.refs_0_, bf16[512,512]{1,0:T(8,128)(2,1)S(1)} %branch_0_fun.13.refs_1_), custom_call_target="tpu_custom_call" | custom-call | tf_op jit(solution)/shard_map/cond/branch_0_fun/pallas_call | solution.py:196
  194.7 4.4 %branch_0_fun.19.refs_8_ = bf16[1,1024,512]{2,1,0:T(8,128)(2,1)S(1)} custom-call(bf16[512,512]{1,0:T(8,128)(2,1)S(1)} %branch_0_fun.17.refs_0_, bf16[512,512]{1,0:T(8,128)(2,1)S(1)} %branch_0_fun.18.refs_1_), custom_call_target="tpu_custom_call" | custom-call | tf_op jit(solution)/shard_map/cond/branch_0_fun/pallas_call | solution.py:196
  199.1 2.4 %branch_0_fun.14 = (bf16[512,1024]{1,0:T(8,128)(2,1)S(1)}, bf16[1024,512]{1,0:T(8,128)(2,1)S(1)}) custom-call(s32[4]{0:T(128)S(1)} %add_multiply_fusion.base_ref, s32[1024,1]{1,0:T(8,128)S(1)} %copy.18.ids_ref, bf16[256,1024]{1,0:T(8,128)(2,1)S(1)} %copy-done.5, bf16[256,1024]{1,0:T(8,128)(2,1)S(1)} %collective-permute-done.3.refs_1_, ...), custom_call_target="tpu_custom_call" | custom-call | tf_op jit(solution)/shard_map/cond/branch_0_fun/pallas_call | solution.py:127
  201.5 12.3 %branch_0_fun.16 = (bf16[1,1024,1024]{2,1,0:T(8,128)(2,1)}, bf16[1,1024,1024]{2,1,0:T(8,128)(2,1)}, f32[256,512]{1,0:T(8,128)S(1)}) custom-call(bf16[512,512]{1,0:T(8,128)(2,1)S(1)} %branch_0_fun.12.refs_0_, bf16[512,512]{1,0:T(8,128)(2,1)S(1)} %branch_0_fun.13.refs_1_, bf16[512,512]{1,0:T(8,128)(2,1)S(1)} %collective-permute-done.9.refs_2_, ...), custom_call_target="tpu_custom_call" | custom-call | tf_op jit(solution)/shard_map/cond/branch_0_fun/pallas_call | solution.py:276
  213.8 12.3 %branch_0_fun.20 = (bf16[1,1024,1024]{2,1,0:T(8,128)(2,1)}, bf16[1,1024,1024]{2,1,0:T(8,128)(2,1)}, f32[256,512]{1,0:T(8,128)S(1)}) custom-call(bf16[512,512]{1,0:T(8,128)(2,1)S(1)} %branch_0_fun.17.refs_0_, bf16[512,512]{1,0:T(8,128)(2,1)S(1)} %branch_0_fun.18.refs_1_, ...), custom_call_target="tpu_custom_call", output_to_operand_aliasing={{0}: (15, {}), {1}: (16, {})} | custom-call | tf_op jit(solution)/shard_map/cond/branch_0_fun/pallas_call | solution.py:276
  226.1 1.0 branch_0_fun.21
  (23 shorter events, 0.1 us)
Async XLA Ops:
  1.3 4.4 %copy-start.3 = (bf16[1024,1024]{1,0:T(8,128)(2,1)S(1)}, bf16[1024,1024]{1,0:T(8,128)(2,1)}, u32[]{:S(2)}) copy-start(bf16[1024,1024]{1,0:T(8,128)(2,1)} %get-tuple-element.24) | copy-start | bytes 6291460 | tf_op jit(solution)/shard_map/cond
  1.3 13.9 %collective-permute-start.4 = (bf16[256,1024]{1,0:T(8,128)(2,1)}, bf16[256,1024]{1,0:T(8,128)(2,1)S(1)}, u32[]{:S(2)}, u32[]{:S(2)}) collective-permute-start(bf16[256,1024]{1,0:T(8,128)(2,1)} %get-tuple-element.28.refs_0_), channel_id=1, source_target_pairs={{0,4},{2,6},{4,0},{6,2},{1,5},{3,7},{5,1},{7,3},{8,12},{10,14},{12... | collective-permute-start | bytes 1572872 | tf_op jit(solution)/shard_map/cond/branch_0_fun/ppermute | solution.py:37
  2.9 13.3 %collective-permute-start.3 = (bf16[256,1024]{1,0:T(8,128)(2,1)}, bf16[256,1024]{1,0:T(8,128)(2,1)S(1)}, u32[]{:S(2)}, u32[]{:S(2)}) collective-permute-start(bf16[256,1024]{1,0:T(8,128)(2,1)} %get-tuple-element.28.refs_0_), channel_id=1, source_target_pairs={{0,2},{2,0},{4,6},{6,4},{1,3},{3,1},{5,7},{7,5},{8,10},{10,8},{12,... | collective-permute-start | bytes 1572872 | tf_op jit(solution)/shard_map/cond/branch_0_fun/ppermute | solution.py:37
  4.2 32.5 %collective-permute-start.6 = (bf16[256,1024]{1,0:T(8,128)(2,1)S(1)}, bf16[256,1024]{1,0:T(8,128)(2,1)S(1)}, u32[]{:S(2)}, u32[]{:S(2)}) collective-permute-start(bf16[256,1024]{1,0:T(8,128)(2,1)S(1)} %get-tuple-element.68.refs_4_), channel_id=1, source_target_pairs={{0,1},{1,0},{2,3},{3,2},{4,5},{5,4},{6,7},{7,6},{8,9},{9,8},{10,11... | collective-permute-start | bytes 1572872 | tf_op jit(solution)/shard_map/cond/branch_0_fun/ppermute | solution.py:37
  5.7 3.9 %copy-start.13 = (s32[2,512]{1,0:T(2,128)S(1)}, s32[2,512]{1,0:T(2,128)}, u32[]{:S(2)}) copy-start(s32[2,512]{1,0:T(2,128)} %get-tuple-element.27) | copy-start | bytes 12292 | tf_op jit(solution)/shard_map/cond
  7.1 17.0 %collective-permute-start.12 = (bf16[256,1024]{1,0:T(8,128)(2,1)}, bf16[256,1024]{1,0:T(8,128)(2,1)}, u32[]{:S(2)}, u32[]{:S(2)}) collective-permute-start(bf16[256,1024]{1,0:T(8,128)(2,1)} %get-tuple-element.62), channel_id=1, source_target_pairs={{0,8},{24,16},{1,9},{25,17},{2,10},{26,18},{3,11},{27,19},{4,12},{... | collective-permute-start | bytes 1572872 | tf_op jit(solution)/shard_map/cond/branch_0_fun/ppermute | solution.py:37
  8.4 26.9 %collective-permute-start.15 = (bf16[256,1024]{1,0:T(8,128)(2,1)}, bf16[256,1024]{1,0:T(8,128)(2,1)}, u32[]{:S(2)}, u32[]{:S(2)}) collective-permute-start(bf16[256,1024]{1,0:T(8,128)(2,1)} %get-tuple-element.61), channel_id=1, source_target_pairs={{0,8},{24,16},{1,9},{25,17},{2,10},{26,18},{3,11},{27,19},{4,12},{... | collective-permute-start | bytes 1572872 | tf_op jit(solution)/shard_map/cond/branch_0_fun/ppermute | solution.py:37
  10.1 6.1 %copy-start.10 = (bf16[256,1024]{1,0:T(8,128)(2,1)S(1)}, bf16[256,1024]{1,0:T(8,128)(2,1)}, u32[]{:S(2)}) copy-start(bf16[256,1024]{1,0:T(8,128)(2,1)} %get-tuple-element.60) | copy-start | bytes 1572868 | tf_op jit(solution)/shard_map/cond
  10.1 14.0 %copy-start.9 = (bf16[256,1024]{1,0:T(8,128)(2,1)S(1)}, bf16[256,1024]{1,0:T(8,128)(2,1)}, u32[]{:S(2)}) copy-start(bf16[256,1024]{1,0:T(8,128)(2,1)} %get-tuple-element.59) | copy-start | bytes 1572868 | tf_op jit(solution)/shard_map/cond
  15.3 31.2 %collective-permute-start.7 = (bf16[512,512]{1,0:T(8,128)(2,1)S(1)}, bf16[512,512]{1,0:T(8,128)(2,1)S(1)}, u32[]{:S(2)}, u32[]{:S(2)}) collective-permute-start(bf16[512,512]{1,0:T(8,128)(2,1)S(1)} %get-tuple-element.66), channel_id=1, source_target_pairs={{0,8},{8,0},{16,24},{24,16},{1,9},{9,1},{17,25},{25,17},{2,10},{10... | collective-permute-start | bytes 1572872 | tf_op jit(solution)/shard_map/cond/branch_0_fun/ppermute | solution.py:37
  16.2 41.5 %collective-permute-start.18 = (bf16[256,1024]{1,0:T(8,128)(2,1)S(1)}, bf16[256,1024]{1,0:T(8,128)(2,1)S(1)}, u32[]{:S(2)}, u32[]{:S(2)}) collective-permute-start(bf16[256,1024]{1,0:T(8,128)(2,1)S(1)} %copy-done.10), channel_id=1, source_target_pairs={{0,8},{24,16},{1,9},{25,17},{2,10},{26,18},{3,11},{27,19},{4,12},{... | collective-permute-start | bytes 1572872 | tf_op jit(solution)/shard_map/cond/branch_0_fun/ppermute | solution.py:37
  24.1 44.8 %collective-permute-start = (bf16[256,1024]{1,0:T(8,128)(2,1)S(1)}, bf16[256,1024]{1,0:T(8,128)(2,1)S(1)}, u32[]{:S(2)}, u32[]{:S(2)}) collective-permute-start(bf16[256,1024]{1,0:T(8,128)(2,1)S(1)} %copy-done.9), channel_id=1, source_target_pairs={{0,8},{24,16},{1,9},{25,17},{2,10},{26,18},{3,11},{27,19},{4,12},{... | collective-permute-start | bytes 1572872 | tf_op jit(solution)/shard_map/cond/branch_0_fun/ppermute | solution.py:37
  26.8 48.4 %copy-start.5 = (bf16[256,1024]{1,0:T(8,128)(2,1)S(1)}, bf16[256,1024]{1,0:T(8,128)(2,1)}, u32[]{:S(2)}) copy-start(bf16[256,1024]{1,0:T(8,128)(2,1)} %get-tuple-element.28.refs_0_) | copy-start | bytes 1572868 | tf_op jit(solution)/shard_map/cond
  35.3 37.3 %collective-permute-start.5 = (bf16[256,1024]{1,0:T(8,128)(2,1)S(1)}, bf16[256,1024]{1,0:T(8,128)(2,1)S(1)}, u32[]{:S(2)}, u32[]{:S(2)}) collective-permute-start(bf16[256,1024]{1,0:T(8,128)(2,1)S(1)} %collective-permute-done.4.refs_2_), channel_id=1, source_target_pairs={{0,2},{2,0},{4,6},{6,4},{1,3},{3,1},{5,7},{7,5},{8,10},{10,8},{12,... | collective-permute-start | bytes 1572872 | tf_op jit(solution)/shard_map/cond/branch_0_fun/ppermute | solution.py:37
  36.7 43.4 %collective-permute-start.8 = (bf16[512,512]{1,0:T(8,128)(2,1)S(1)}, bf16[512,512]{1,0:T(8,128)(2,1)S(1)}, u32[]{:S(2)}, u32[]{:S(2)}) collective-permute-start(bf16[512,512]{1,0:T(8,128)(2,1)S(1)} %get-tuple-element.63), channel_id=1, source_target_pairs={{0,8},{8,0},{16,24},{24,16},{1,9},{9,1},{17,25},{25,17},{2,10},{10... | collective-permute-start | bytes 1572872 | tf_op jit(solution)/shard_map/cond/branch_0_fun/ppermute | solution.py:37
  46.4 44.9 %collective-permute-start.22 = (bf16[512,512]{1,0:T(8,128)(2,1)S(1)}, bf16[512,512]{1,0:T(8,128)(2,1)S(1)}, u32[]{:S(2)}, u32[]{:S(2)}) collective-permute-start(bf16[512,512]{1,0:T(8,128)(2,1)S(1)} %get-tuple-element.64), channel_id=1, source_target_pairs={{0,8},{8,0},{16,24},{24,16},{1,9},{9,1},{17,25},{25,17},{2,10},{10... | collective-permute-start | bytes 1572872 | tf_op jit(solution)/shard_map/cond/branch_0_fun/ppermute | solution.py:37
  57.7 44.2 %collective-permute-start.21 = (bf16[512,512]{1,0:T(8,128)(2,1)S(1)}, bf16[512,512]{1,0:T(8,128)(2,1)S(1)}, u32[]{:S(2)}, u32[]{:S(2)}) collective-permute-start(bf16[512,512]{1,0:T(8,128)(2,1)S(1)} %get-tuple-element.65), channel_id=1, source_target_pairs={{0,8},{8,0},{16,24},{24,16},{1,9},{9,1},{17,25},{25,17},{2,10},{10... | collective-permute-start | bytes 1572872 | tf_op jit(solution)/shard_map/cond/branch_0_fun/ppermute | solution.py:37
  68.9 38.3 %collective-permute-start.13 = (bf16[256,1024]{1,0:T(8,128)(2,1)S(1)}, bf16[256,1024]{1,0:T(8,128)(2,1)S(1)}, u32[]{:S(2)}, u32[]{:S(2)}) collective-permute-start(bf16[256,1024]{1,0:T(8,128)(2,1)S(1)} %add_convert_fusion.2), channel_id=1, source_target_pairs={{8,16},{16,8},{9,17},{17,9},{10,18},{18,10},{11,19},{19,11},{12,20... | collective-permute-start | bytes 1572872 | tf_op jit(solution)/shard_map/cond/branch_0_fun/ppermute | solution.py:37
  72.6 34.9 %collective-permute-start.16 = (bf16[256,1024]{1,0:T(8,128)(2,1)S(1)}, bf16[256,1024]{1,0:T(8,128)(2,1)S(1)}, u32[]{:S(2)}, u32[]{:S(2)}) collective-permute-start(bf16[256,1024]{1,0:T(8,128)(2,1)S(1)} %add_convert_fusion.1), channel_id=1, source_target_pairs={{8,16},{16,8},{9,17},{17,9},{10,18},{18,10},{11,19},{19,11},{12,20... | collective-permute-start | bytes 1572872 | tf_op jit(solution)/shard_map/cond/branch_0_fun/ppermute | solution.py:37
  80.1 32.1 %collective-permute-start.11 = (bf16[256,1024]{1,0:T(8,128)(2,1)S(1)}, bf16[256,1024]{1,0:T(8,128)(2,1)S(1)}, u32[]{:S(2)}, u32[]{:S(2)}) collective-permute-start(bf16[256,1024]{1,0:T(8,128)(2,1)S(1)} %get-tuple-element.67.refs_4_), channel_id=1, source_target_pairs={{0,1},{1,0},{2,3},{3,2},{4,5},{5,4},{6,7},{7,6},{8,9},{9,8},{10,11... | collective-permute-start | bytes 1572872 | tf_op jit(solution)/shard_map/cond/branch_0_fun/ppermute | solution.py:37
  91.4 19.3 %collective-permute-start.19 = (bf16[256,1024]{1,0:T(8,128)(2,1)S(1)}, bf16[256,1024]{1,0:T(8,128)(2,1)S(1)}, u32[]{:S(2)}, u32[]{:S(2)}) collective-permute-start(bf16[256,1024]{1,0:T(8,128)(2,1)S(1)} %add_convert_fusion), channel_id=1, source_target_pairs={{8,16},{16,8},{9,17},{17,9},{10,18},{18,10},{11,19},{19,11},{12,20... | collective-permute-start | bytes 1572872 | tf_op jit(solution)/shard_map/cond/branch_0_fun/ppermute | solution.py:37
  101.9 39.1 %collective-permute-start.1 = (bf16[256,1024]{1,0:T(8,128)(2,1)S(1)}, bf16[256,1024]{1,0:T(8,128)(2,1)S(1)}, u32[]{:S(2)}, u32[]{:S(2)}) collective-permute-start(bf16[256,1024]{1,0:T(8,128)(2,1)S(1)} %add_convert_fusion.3), channel_id=1, source_target_pairs={{8,16},{16,8},{9,17},{17,9},{10,18},{18,10},{11,19},{19,11},{12,20... | collective-permute-start | bytes 1572872 | tf_op jit(solution)/shard_map/cond/branch_0_fun/ppermute | solution.py:37
  107.2 55.3 %collective-permute-start.10 = (bf16[512,512]{1,0:T(8,128)(2,1)S(1)}, bf16[512,512]{1,0:T(8,128)(2,1)S(1)}, u32[]{:S(2)}, u32[]{:S(2)}) collective-permute-start(bf16[512,512]{1,0:T(8,128)(2,1)S(1)} %branch_0_fun.13.refs_1_), channel_id=1, source_target_pairs={{0,16},{8,24},{16,0},{24,8},{1,17},{9,25},{17,1},{25,9},{2,18},{10... | collective-permute-start | bytes 1572872 | tf_op jit(solution)/shard_map/cond/branch_0_fun/ppermute | solution.py:37
  107.5 77.6 %collective-permute-start.9 = (bf16[512,512]{1,0:T(8,128)(2,1)S(1)}, bf16[512,512]{1,0:T(8,128)(2,1)S(1)}, u32[]{:S(2)}, u32[]{:S(2)}) collective-permute-start(bf16[512,512]{1,0:T(8,128)(2,1)S(1)} %branch_0_fun.12.refs_0_), channel_id=1, source_target_pairs={{0,16},{8,24},{16,0},{24,8},{1,17},{9,25},{17,1},{25,9},{2,18},{10... | collective-permute-start | bytes 1572872 | tf_op jit(solution)/shard_map/cond/branch_0_fun/ppermute | solution.py:37
  110.7 78.1 %collective-permute-start.14 = (bf16[256,1024]{1,0:T(8,128)(2,1)S(1)}, bf16[256,1024]{1,0:T(8,128)(2,1)S(1)}, u32[]{:S(2)}, u32[]{:S(2)}) collective-permute-start(bf16[256,1024]{1,0:T(8,128)(2,1)S(1)} %multiply_convert_fusion.2.refs_9_), channel_id=1, source_target_pairs={{8,0},{16,24},{9,1},{17,25},{10,2},{18,26},{11,3},{19,27},{12,4},{... | collective-permute-start | bytes 1572872 | tf_op jit(solution)/shard_map/cond/branch_0_fun/ppermute | solution.py:37
  112.3 89.2 %collective-permute-start.17 = (bf16[256,1024]{1,0:T(8,128)(2,1)S(1)}, bf16[256,1024]{1,0:T(8,128)(2,1)S(1)}, u32[]{:S(2)}, u32[]{:S(2)}) collective-permute-start(bf16[256,1024]{1,0:T(8,128)(2,1)S(1)} %multiply_convert_fusion.1.refs_11_), channel_id=1, source_target_pairs={{8,0},{16,24},{9,1},{17,25},{10,2},{18,26},{11,3},{19,27},{12,4},{... | collective-permute-start | bytes 1572872 | tf_op jit(solution)/shard_map/cond/branch_0_fun/ppermute | solution.py:37
  141.0 60.4 %collective-permute-start.20 = (bf16[256,1024]{1,0:T(8,128)(2,1)S(1)}, bf16[256,1024]{1,0:T(8,128)(2,1)S(1)}, u32[]{:S(2)}, u32[]{:S(2)}) collective-permute-start(bf16[256,1024]{1,0:T(8,128)(2,1)S(1)} %multiply_convert_fusion.refs_13_), channel_id=1, source_target_pairs={{8,0},{16,24},{9,1},{17,25},{10,2},{18,26},{11,3},{19,27},{12,4},{... | collective-permute-start | bytes 1572872 | tf_op jit(solution)/shard_map/cond/branch_0_fun/ppermute | solution.py:37
  162.5 51.3 %collective-permute-start.24 = (bf16[512,512]{1,0:T(8,128)(2,1)S(1)}, bf16[512,512]{1,0:T(8,128)(2,1)S(1)}, u32[]{:S(2)}, u32[]{:S(2)}) collective-permute-start(bf16[512,512]{1,0:T(8,128)(2,1)S(1)} %branch_0_fun.18.refs_1_), channel_id=1, source_target_pairs={{0,16},{8,24},{16,0},{24,8},{1,17},{9,25},{17,1},{25,9},{2,18},{10... | collective-permute-start | bytes 1572872 | tf_op jit(solution)/shard_map/cond/branch_0_fun/ppermute | solution.py:37
  185.2 28.6 %collective-permute-start.23 = (bf16[512,512]{1,0:T(8,128)(2,1)S(1)}, bf16[512,512]{1,0:T(8,128)(2,1)S(1)}, u32[]{:S(2)}, u32[]{:S(2)}) collective-permute-start(bf16[512,512]{1,0:T(8,128)(2,1)S(1)} %branch_0_fun.17.refs_0_), channel_id=1, source_target_pairs={{0,16},{8,24},{16,0},{24,8},{1,17},{9,25},{17,1},{25,9},{2,18},{10... | collective-permute-start | bytes 1572872 | tf_op jit(solution)/shard_map/cond/branch_0_fun/ppermute | solution.py:37
  188.8 37.3 %collective-permute-start.2 = (bf16[256,1024]{1,0:T(8,128)(2,1)S(1)}, bf16[256,1024]{1,0:T(8,128)(2,1)S(1)}, u32[]{:S(2)}, u32[]{:S(2)}) collective-permute-start(bf16[256,1024]{1,0:T(8,128)(2,1)S(1)} %multiply_convert_fusion.3.refs_0_), channel_id=1, source_target_pairs={{8,0},{16,24},{9,1},{17,25},{10,2},{18,26},{11,3},{19,27},{12,4},{... | collective-permute-start | bytes 1572872 | tf_op jit(solution)/shard_map/cond/branch_0_fun/ppermute | solution.py:37

commit v3 on v2

--- a/solution.py
+++ b/solution.py
@@ -15,7 +15,7 @@
 NS_ITERS = 2
 STEPS = 2
 SPLIT = 2
-NEAR_PLAN = ((4, 4, 4, 4), 3, False)
+NEAR_PLAN = ((4, 4, 4, 4), 4, False)
 FAR_PLAN = ((4, 4, 4, 4), 2, True)
 TILE = 256
 
@@ -185,25 +185,36 @@
     loop(count, scale)
 
 
-def orthogonal(pieces):
+def orthogonal(pieces, grads, block):
     height, width = pieces[0].shape
     height *= len(pieces)
+    cut = slice(block * width, (block + 1) * width)
 
     def kernel(*refs):
-        refs[-1][0] = stacked(refs[:-1])
-        newton_schulz(refs[-1], 1)
-
-    return call(kernel, jax.ShapeDtypeStruct((1, height, width), bf16))(*pieces)
+        turned_1, chosen_1, turned_0, chosen_0, x_ref, base_ref = refs[len(pieces) :]
+        x_ref[0] = stacked(refs[: len(pieces)])
+
+        def mix(k):
+            t = tile(k, TILE)
+            fresh = dot(turned_1[t, :], chosen_1[:, cut]) - dot(turned_0[t, :], chosen_0[:, cut])
+            base_ref[t, :] = 0.5 * x_ref[0, t, :].astype(f32) + fresh
+
+        loop(height // TILE, mix)
+        newton_schulz(x_ref, 1)
+
+    out_shape = (
+        jax.ShapeDtypeStruct((1, height, width), bf16),
+        jax.ShapeDtypeStruct((height, width), f32),
+    )
+    return call(kernel, out_shape, mib=16)(*pieces, *grads)
 
 
 def sliver(*sizes):
     return math.gcd(64, *sizes)
 
 
-def second_mix(mine, theirs, grads, first, means, scale, block, whole, previous):
-    pieces = len(mine)
-    height, width = mine[0].shape
-    height *= pieces
+def second_mix(theirs, base, first, means, scale, block, whole, previous):
+    height, width = base.shape
     sizes = [parts[0].shape[0] for parts in means]
     early = sum(sizes)
     flat = [part for parts in means for part in parts]
@@ -213,19 +224,15 @@
     outs = 3 if early < height else 2
 
     def kernel(*refs):
-        mine_refs, refs = refs[:pieces], refs[pieces:]
+        *out_refs, x_ref, tracker_ref, weights_ref, sems = refs[-outs - 4 :]
         theirs_refs, refs = refs[: len(received)], refs[len(received) :]
-        turned_1, chosen_1, turned_0, chosen_0, first_ref = refs[:5]
-        mean_refs = refs[5 : 5 + len(flat)]
-        *out_refs, x_ref, y_ref, tracker_ref, weights_ref, sems = refs[-outs - 5 :]
+        base_ref, first_ref = refs[:2]
+        mean_refs = refs[2 : 2 + len(flat)]
         x_ref[0] = sum(stacked(theirs_refs[part::parts]) for part in range(parts))
-        y_ref[...] = stacked(mine_refs)
 
         def mix(k):
             t = tile(k, TILE)
-            fresh = dot(turned_1[t, :], chosen_1[:, cut]) - dot(turned_0[t, :], chosen_0[:, cut])
-            mean = 0.5 * (y_ref[t, :].astype(f32) + x_ref[0, t, :].astype(f32))
-            mixed = (mean + fresh).astype(bf16)
+            mixed = (base_ref[t, :] + 0.5 * x_ref[0, t, :].astype(f32)).astype(bf16)
             tracker_ref[t, :] = mixed
             x_ref[1, t, :] = mixed
 
@@ -263,7 +270,7 @@
 
     vmem = pl.BlockSpec(memory_space=pltpu.VMEM)
     apart = pl.BlockSpec(memory_space=pltpu.HBM)
-    operands = [*mine, *received, *grads, first, *flat]
+    operands = [*received, base, first, *flat]
     in_specs = [vmem] * len(operands)
     aliases = {}
     if previous is not None:
@@ -282,7 +289,6 @@
         scratch_shapes=[
             pltpu.VMEM((2, height, width), bf16),
             pltpu.VMEM((height, width), bf16),
-            pltpu.VMEM((height, width), bf16),
             pltpu.VMEM((early, width), bf16),
             pltpu.SemaphoreType.DMA((2,)),
         ],
@@ -375,19 +381,19 @@
             mixed = first_mix(tracker, others, grad_prev, *grads[2:], r, col, piece, width)
             mine[-1].append(mixed)
             theirs[-1].append(swap(mixed, second_mask, relay))
-    first = [orthogonal(mine[col]) for col in range(len(mine))]
+    own = [orthogonal(mine[col], grads, col) for col in range(len(mine))]
 
     ends = [rows * sum(shares[: k + 1]) // sum(shares) for k in range(len(shares))]
     cuts = list(zip([0, *ends], ends))
     means = []
     for k, (low, high) in enumerate(cuts):
-        own = lax.optimization_barrier(lax.slice_in_dim(weights, low, high))
-        means.append(mean_of_four(own, first_route, second_route))
+        rows_here = lax.optimization_barrier(lax.slice_in_dim(weights, low, high))
+        means.append(mean_of_four(rows_here, first_route, second_route))
 
     results, updates = None, []
     for col in range(cols // width):
         *results, update = *second_mix(
-            mine[col], theirs[col], grads, first[col], means[:early], scale, col,
+            theirs[col], own[col][1], own[col][0], means[:early], scale, col,
             weights.shape, results,
         ), None
         if early < len(shares):

time: 228 us -> 254 us (1.11)
  the two profiles are of different devices: /device:TPU:8 before, /device:TPU:0 now
where the time goes in v3:
time: 254 us
  waiting for transfers between devices  127 us (50%)
  starting transfers between devices  68.6 us (27%)
  Pallas kernels  45.2 us (18%)
  local copies, waits for them, and re-layouts  6.69 us (3%)
  other arithmetic  4.03 us (2%)
    ppermute x25, waiting for transfers between devices, send(): return lax.ppermute(x, axis, route)  127 us
    ppermute x25, starting transfers between devices, send(): return lax.ppermute(x, axis, route)  68.6 us
    pallas_call x2, Pallas kernels, second_mix(): call(kernel, mib=24, out_shape=out_shape, in_specs=in_specs, out_specs=[a...  20.7 us
    pallas_call x2, Pallas kernels, orthogonal(): return call(kernel, out_shape, mib=16)(*pieces, *grads)  12.4 us
    pallas_call x4, Pallas kernels, first_mix(): call(kernel, jax.ShapeDtypeStruct((height, width), bf16), grid=(1,), in_s...  7.44 us
  transfers between devices with their start and end apart: 25, of which 12 were waited for; matrix products, arithmetic and copies ran while one was open for 3% of the time, Pallas kernels for 14%

profile of v3, /device:TPU:0, one launch (start us, length us, event | category | flops | bytes accessed | tf_op | source)
XLA Modules:
  0.0 253.6 jit_solution(441555714318041494)
XLA Ops:
  1.3 252.3 %conditional.1 = (bf16[1,1024,1024]{2,1,0:T(8,128)(2,1)}, bf16[1,1024,1024]{2,1,0:T(8,128)(2,1)}) conditional(s32[]{:T(128)} %clamp.3, (s32[2,512]{1,0:T(2,128)}, bf16[256,1024]{1,0:T(8,128)(2,1)}, bf16[2,256,1024]{2,1,0:T(8,128)(2,1)}, bf16[1024,1024]{1,0:T(8,128)(2,1)}, bf16[1024,1024]{1,0:T(8,128)(2,1)}, ...), branch_computations={%region_0.1_spmd, %region_1.2_spmd} | conditional | flops 9440296 | bytes 161523952 | solution.py:414
  1.3 0.0 copy-start.5
  1.3 3.1 %collective-permute-start.1 = (bf16[256,1024]{1,0:T(8,128)(2,1)}, bf16[256,1024]{1,0:T(8,128)(2,1)S(1)}, u32[]{:S(2)}, u32[]{:S(2)}) collective-permute-start(bf16[256,1024]{1,0:T(8,128)(2,1)} %get-tuple-element.27.refs_0_), channel_id=1, source_target_pairs={{0,4},{2,6},{4,0},{6,2},{1,5},{3,7},{5,1},{7,3},{8,12},{10,14},{12... | collective-permute-start | bytes 1572872 | tf_op jit(solution)/shard_map/cond/branch_0_fun/ppermute | solution.py:37
  4.4 1.3 slice_bitcast_fusion
  5.7 1.6 collective-permute-start.3
  7.2 1.4 fusion.1
  8.6 4.3 %collective-permute-start.9 = (bf16[256,1024]{1,0:T(8,128)(2,1)}, bf16[256,1024]{1,0:T(8,128)(2,1)}, u32[]{:S(2)}, u32[]{:S(2)}) collective-permute-start(bf16[256,1024]{1,0:T(8,128)(2,1)} %get-tuple-element.71), channel_id=1, source_target_pairs={{0,8},{24,16},{1,9},{25,17},{2,10},{26,18},{3,11},{27,19},{4,12},{... | collective-permute-start | bytes 1572872 | tf_op jit(solution)/shard_map/cond/branch_0_fun/ppermute | solution.py:37
  12.9 2.1 collective-permute-start.12
  15.0 0.1 constant_dynamic-slice_fusion.1
  15.1 0.2 copy.15.ids_ref
  15.3 0.1 add_multiply_fusion.base_ref
  15.4 1.7 fusion
  17.1 3.1 %collective-permute-start.15 = (bf16[256,1024]{1,0:T(8,128)(2,1)S(1)}, bf16[256,1024]{1,0:T(8,128)(2,1)S(1)}, u32[]{:S(2)}, u32[]{:S(2)}) collective-permute-start(bf16[256,1024]{1,0:T(8,128)(2,1)S(1)} %copy-done.12), channel_id=1, source_target_pairs={{0,8},{24,16},{1,9},{25,17},{2,10},{26,18},{3,11},{27,19},{4,12},{... | collective-permute-start | bytes 1572872 | tf_op jit(solution)/shard_map/cond/branch_0_fun/ppermute | solution.py:37
  20.2 4.4 %collective-permute-done.9 = bf16[256,1024]{1,0:T(8,128)(2,1)} collective-permute-done((bf16[256,1024]{1,0:T(8,128)(2,1)}, bf16[256,1024]{1,0:T(8,128)(2,1)}, u32[]{:S(2)}, u32[]{:S(2)}) %collective-permute-start.9) | collective-permute-done | bytes 524320 | tf_op jit(solution)/shard_map/cond/branch_0_fun/ppermute | solution.py:37
  24.7 4.4 %collective-permute-start.18 = (bf16[256,1024]{1,0:T(8,128)(2,1)S(1)}, bf16[256,1024]{1,0:T(8,128)(2,1)S(1)}, u32[]{:S(2)}, u32[]{:S(2)}) collective-permute-start(bf16[256,1024]{1,0:T(8,128)(2,1)S(1)} %copy-done.11), channel_id=1, source_target_pairs={{0,8},{24,16},{1,9},{25,17},{2,10},{26,18},{3,11},{27,19},{4,12},{... | collective-permute-start | bytes 1572872 | tf_op jit(solution)/shard_map/cond/branch_0_fun/ppermute | solution.py:37
  29.1 1.4 add_convert_fusion.3
  30.5 5.4 %collective-permute-done.12 = bf16[256,1024]{1,0:T(8,128)(2,1)} collective-permute-done((bf16[256,1024]{1,0:T(8,128)(2,1)}, bf16[256,1024]{1,0:T(8,128)(2,1)}, u32[]{:S(2)}, u32[]{:S(2)}) %collective-permute-start.12) | collective-permute-done | bytes 524320 | tf_op jit(solution)/shard_map/cond/branch_0_fun/ppermute | solution.py:37
  35.9 1.4 add_convert_fusion.2
  37.3 2.5 %collective-permute-start.21 = (bf16[512,512]{1,0:T(8,128)(2,1)S(1)}, bf16[512,512]{1,0:T(8,128)(2,1)S(1)}, u32[]{:S(2)}, u32[]{:S(2)}) collective-permute-start(bf16[512,512]{1,0:T(8,128)(2,1)S(1)} %get-tuple-element.65), channel_id=1, source_target_pairs={{0,8},{8,0},{16,24},{24,16},{1,9},{9,1},{17,25},{25,17},{2,10},{10... | collective-permute-start | bytes 1572872 | tf_op jit(solution)/shard_map/cond/branch_0_fun/ppermute | solution.py:37
  39.9 0.1 collective-permute-start.23
  40.0 7.1 %collective-permute-done.15 = bf16[256,1024]{1,0:T(8,128)(2,1)S(1)} collective-permute-done((bf16[256,1024]{1,0:T(8,128)(2,1)S(1)}, bf16[256,1024]{1,0:T(8,128)(2,1)S(1)}, u32[]{:S(2)}, u32[]{:S(2)}) %collective-permute-start.15) | collective-permute-done | bytes 524320 | tf_op jit(solution)/shard_map/cond/branch_0_fun/ppermute | solution.py:37
  47.0 2.5 collective-permute-start.6
  49.5 8.8 %collective-permute-done.18 = bf16[256,1024]{1,0:T(8,128)(2,1)S(1)} collective-permute-done((bf16[256,1024]{1,0:T(8,128)(2,1)S(1)}, bf16[256,1024]{1,0:T(8,128)(2,1)S(1)}, u32[]{:S(2)}, u32[]{:S(2)}) %collective-permute-start.18) | collective-permute-done | bytes 524320 | tf_op jit(solution)/shard_map/cond/branch_0_fun/ppermute | solution.py:37
  58.3 0.7 collective-permute-start.10
  59.0 0.2 add_convert_fusion.1
  59.2 0.7 collective-permute-start.13
  59.9 0.2 add_convert_fusion
  60.1 2.4 branch_0_fun.10
  62.5 7.1 %collective-permute-done.21.refs_0_ = bf16[512,512]{1,0:T(8,128)(2,1)S(1)} collective-permute-done((bf16[512,512]{1,0:T(8,128)(2,1)S(1)}, bf16[512,512]{1,0:T(8,128)(2,1)S(1)}, u32[]{:S(2)}, u32[]{:S(2)}) %collective-permute-start.21) | collective-permute-done | bytes 524320 | tf_op jit(solution)/shard_map/cond/branch_0_fun/ppermute | solution.py:37
  69.5 0.5 collective-permute-start.8
  70.0 1.9 branch_0_fun.15.refs_0_
  71.9 8.8 %collective-permute-done.23.refs_0_ = bf16[512,512]{1,0:T(8,128)(2,1)S(1)} collective-permute-done((bf16[512,512]{1,0:T(8,128)(2,1)S(1)}, bf16[512,512]{1,0:T(8,128)(2,1)S(1)}, u32[]{:S(2)}, u32[]{:S(2)}) %collective-permute-start.23) | collective-permute-done | bytes 524320 | tf_op jit(solution)/shard_map/cond/branch_0_fun/ppermute | solution.py:37
  80.7 2.5 collective-permute-start.4
  83.2 1.9 branch_0_fun.16.refs_1_
  85.1 6.9 %collective-permute-done.6.refs_0_ = bf16[512,512]{1,0:T(8,128)(2,1)S(1)} collective-permute-done((bf16[512,512]{1,0:T(8,128)(2,1)S(1)}, bf16[512,512]{1,0:T(8,128)(2,1)S(1)}, u32[]{:S(2)}, u32[]{:S(2)}) %collective-permute-start.6) | collective-permute-done | bytes 524320 | tf_op jit(solution)/shard_map/cond/branch_0_fun/ppermute | solution.py:37
  92.0 0.7 collective-permute-start.16
  92.7 1.9 branch_0_fun.12.refs_1_
  94.5 0.7 collective-permute-start.19
  95.2 0.2 multiply_convert_fusion.3.refs_4_
  95.5 8.0 %collective-permute-start.22 = (bf16[512,512]{1,0:T(8,128)(2,1)S(1)}, bf16[512,512]{1,0:T(8,128)(2,1)S(1)}, u32[]{:S(2)}, u32[]{:S(2)}) collective-permute-start(bf16[512,512]{1,0:T(8,128)(2,1)S(1)} %branch_0_fun.15.refs_0_), channel_id=1, source_target_pairs={{0,16},{8,24},{16,0},{24,8},{1,17},{9,25},{17,1},{25,9},{2,18},{10... | collective-permute-start | bytes 1572872 | tf_op jit(solution)/shard_map/cond/branch_0_fun/ppermute | solution.py:37
  103.5 0.2 multiply_convert_fusion.2.refs_6_
  103.7 25.3 %collective-permute-start.24 = (bf16[512,512]{1,0:T(8,128)(2,1)S(1)}, bf16[512,512]{1,0:T(8,128)(2,1)S(1)}, u32[]{:S(2)}, u32[]{:S(2)}) collective-permute-start(bf16[512,512]{1,0:T(8,128)(2,1)S(1)} %branch_0_fun.16.refs_1_), channel_id=1, source_target_pairs={{0,16},{8,24},{16,0},{24,8},{1,17},{9,25},{17,1},{25,9},{2,18},{10... | collective-permute-start | bytes 1572872 | tf_op jit(solution)/shard_map/cond/branch_0_fun/ppermute | solution.py:37
  129.0 1.3 collective-permute-start.11
  130.3 0.2 multiply_convert_fusion.1.refs_8_
  130.5 0.2 multiply_convert_fusion.refs_10_
  130.7 1.3 collective-permute-start.14
  132.0 1.3 collective-permute-start.17
  133.3 22.3 %collective-permute-done.22.refs_0_ = bf16[512,512]{1,0:T(8,128)(2,1)S(1)} collective-permute-done((bf16[512,512]{1,0:T(8,128)(2,1)S(1)}, bf16[512,512]{1,0:T(8,128)(2,1)S(1)}, u32[]{:S(2)}, u32[]{:S(2)}) %collective-permute-start.22) | collective-permute-done | bytes 524320 | tf_op jit(solution)/shard_map/cond/branch_0_fun/ppermute | solution.py:37
  155.6 1.5 collective-permute-start.20
  157.1 1.9 branch_0_fun.11.refs_0_
  159.0 5.6 %collective-permute-done.24.refs_1_ = bf16[512,512]{1,0:T(8,128)(2,1)S(1)} collective-permute-done((bf16[512,512]{1,0:T(8,128)(2,1)S(1)}, bf16[512,512]{1,0:T(8,128)(2,1)S(1)}, u32[]{:S(2)}, u32[]{:S(2)}) %collective-permute-start.24) | collective-permute-done | bytes 524320 | tf_op jit(solution)/shard_map/cond/branch_0_fun/ppermute | solution.py:37
  164.5 11.3 %collective-permute-done.11.refs_5_ = bf16[256,1024]{1,0:T(8,128)(2,1)S(1)} collective-permute-done((bf16[256,1024]{1,0:T(8,128)(2,1)S(1)}, bf16[256,1024]{1,0:T(8,128)(2,1)S(1)}, u32[]{:S(2)}, u32[]{:S(2)}) %collective-permute-start.11) | collective-permute-done | bytes 524320 | tf_op jit(solution)/shard_map/cond/branch_0_fun/ppermute | solution.py:37
  175.8 0.5 collective-permute-start.5
  176.4 2.4 branch_0_fun.13
  178.7 6.2 %branch_0_fun.17 = (bf16[1,1024,512]{2,1,0:T(8,128)(2,1)S(1)}, f32[1024,512]{1,0:T(8,128)S(1)}) custom-call(bf16[512,512]{1,0:T(8,128)(2,1)S(1)} %branch_0_fun.15.refs_0_, bf16[512,512]{1,0:T(8,128)(2,1)S(1)} %branch_0_fun.16.refs_1_, bf16[1024,512]{1,0:T(8,128)(2,1)S(1)} %get-tuple-element.31.refs_2_, bf16[512,1024]{1,0:T(8,128)(2,1)S(1)} %get-tuple-element.32.refs_3_, ...), custom_call_target="tpu_custom_call" | custom-call | tf_op jit(solution)/shard_map/cond/branch_0_fun/pallas_call | solution.py:209
  184.9 6.2 %branch_0_fun.14 = (bf16[1,1024,512]{2,1,0:T(8,128)(2,1)S(1)}, f32[1024,512]{1,0:T(8,128)S(1)}) custom-call(bf16[512,512]{1,0:T(8,128)(2,1)S(1)} %branch_0_fun.11.refs_0_, bf16[512,512]{1,0:T(8,128)(2,1)S(1)} %branch_0_fun.12.refs_1_, bf16[1024,512]{1,0:T(8,128)(2,1)S(1)} %get-tuple-element.31.refs_2_, bf16[512,1024]{1,0:T(8,128)(2,1)S(1)} %get-tuple-element.32.refs_3_, ...), custom_call_target="tpu_custom_call" | custom-call | tf_op jit(solution)/shard_map/cond/branch_0_fun/pallas_call | solution.py:209
  191.2 29.5 %collective-permute-done.17.refs_9_ = bf16[256,1024]{1,0:T(8,128)(2,1)S(1)} collective-permute-done((bf16[256,1024]{1,0:T(8,128)(2,1)S(1)}, bf16[256,1024]{1,0:T(8,128)(2,1)S(1)}, u32[]{:S(2)}, u32[]{:S(2)}) %collective-permute-start.17) | collective-permute-done | bytes 524320 | tf_op jit(solution)/shard_map/cond/branch_0_fun/ppermute | solution.py:37
  220.7 10.2 %collective-permute-done.20.refs_11_ = bf16[256,1024]{1,0:T(8,128)(2,1)S(1)} collective-permute-done((bf16[256,1024]{1,0:T(8,128)(2,1)S(1)}, bf16[256,1024]{1,0:T(8,128)(2,1)S(1)}, u32[]{:S(2)}, u32[]{:S(2)}) %collective-permute-start.20) | collective-permute-done | bytes 524320 | tf_op jit(solution)/shard_map/cond/branch_0_fun/ppermute | solution.py:37
  230.9 10.3 %branch_0_fun.18 = (bf16[1,1024,1024]{2,1,0:T(8,128)(2,1)S(1)}, bf16[1,1024,1024]{2,1,0:T(8,128)(2,1)S(1)}) custom-call(bf16[512,512]{1,0:T(8,128)(2,1)S(1)} %collective-permute-done.22.refs_0_, bf16[512,512]{1,0:T(8,128)(2,1)S(1)} %collective-permute-done.24.refs_1_, f32[1024,512]{1,0:T(8,128)S(1)} %get-tuple-element.36.refs_2_, ...), custom_call_target="tpu_custom_call" | custom-call | tf_op jit(solution)/shard_map/cond/branch_0_fun/pallas_call | solution.py:283
  241.2 10.3 %branch_0_fun.19 = (bf16[1,1024,1024]{2,1,0:T(8,128)(2,1)S(1)}, bf16[1,1024,1024]{2,1,0:T(8,128)(2,1)S(1)}) custom-call(bf16[512,512]{1,0:T(8,128)(2,1)S(1)} %collective-permute-done.5.refs_0_, bf16[512,512]{1,0:T(8,128)(2,1)S(1)} %collective-permute-done.7.refs_1_, ...), custom_call_target="tpu_custom_call", output_to_operand_aliasing={{0}: (12, {}), {1}: (13, {})} | custom-call | tf_op jit(solution)/shard_map/cond/branch_0_fun/pallas_call | solution.py:283
  251.6 0.0 copy-start.3
  251.6 0.0 copy-start.7
  251.6 1.3 copy-done.3
  252.9 0.7 copy-done.7
  (26 shorter events, 0.1 us)
Async XLA Ops:
  1.3 5.9 %copy-start.5 = (bf16[1024,1024]{1,0:T(8,128)(2,1)S(1)}, bf16[1024,1024]{1,0:T(8,128)(2,1)}, u32[]{:S(2)}) copy-start(bf16[1024,1024]{1,0:T(8,128)(2,1)} %get-tuple-element.35) | copy-start | bytes 6291460 | tf_op jit(solution)/shard_map/cond
  1.3 15.8 %collective-permute-start.1 = (bf16[256,1024]{1,0:T(8,128)(2,1)}, bf16[256,1024]{1,0:T(8,128)(2,1)S(1)}, u32[]{:S(2)}, u32[]{:S(2)}) collective-permute-start(bf16[256,1024]{1,0:T(8,128)(2,1)} %get-tuple-element.27.refs_0_), channel_id=1, source_target_pairs={{0,4},{2,6},{4,0},{6,2},{1,5},{3,7},{5,1},{7,3},{8,12},{10,14},{12... | collective-permute-start | bytes 1572872 | tf_op jit(solution)/shard_map/cond/branch_0_fun/ppermute | solution.py:37
  4.4 32.9 %collective-permute-start = (bf16[256,1024]{1,0:T(8,128)(2,1)}, bf16[256,1024]{1,0:T(8,128)(2,1)S(1)}, u32[]{:S(2)}, u32[]{:S(2)}) collective-permute-start(bf16[256,1024]{1,0:T(8,128)(2,1)} %get-tuple-element.27.refs_0_), channel_id=1, source_target_pairs={{0,2},{2,0},{4,6},{6,4},{1,3},{3,1},{5,7},{7,5},{8,10},{10,8},{12,... | collective-permute-start | bytes 1572872 | tf_op jit(solution)/shard_map/cond/branch_0_fun/ppermute | solution.py:37
  5.7 34.2 %collective-permute-start.3 = (bf16[256,1024]{1,0:T(8,128)(2,1)S(1)}, bf16[256,1024]{1,0:T(8,128)(2,1)S(1)}, u32[]{:S(2)}, u32[]{:S(2)}) collective-permute-start(bf16[256,1024]{1,0:T(8,128)(2,1)S(1)} %get-tuple-element.73.refs_4_), channel_id=1, source_target_pairs={{0,1},{1,0},{2,3},{3,2},{4,5},{5,4},{6,7},{7,6},{8,9},{9,8},{10,11... | collective-permute-start | bytes 1572872 | tf_op jit(solution)/shard_map/cond/branch_0_fun/ppermute | solution.py:37
  7.2 7.8 %copy-start.13 = (s32[2,512]{1,0:T(2,128)S(1)}, s32[2,512]{1,0:T(2,128)}, u32[]{:S(2)}) copy-start(s32[2,512]{1,0:T(2,128)} %get-tuple-element.26) | copy-start | bytes 12292 | tf_op jit(solution)/shard_map/cond
  8.6 16.1 %collective-permute-start.9 = (bf16[256,1024]{1,0:T(8,128)(2,1)}, bf16[256,1024]{1,0:T(8,128)(2,1)}, u32[]{:S(2)}, u32[]{:S(2)}) collective-permute-start(bf16[256,1024]{1,0:T(8,128)(2,1)} %get-tuple-element.71), channel_id=1, source_target_pairs={{0,8},{24,16},{1,9},{25,17},{2,10},{26,18},{3,11},{27,19},{4,12},{... | collective-permute-start | bytes 1572872 | tf_op jit(solution)/shard_map/cond/branch_0_fun/ppermute | solution.py:37
  12.9 23.0 %collective-permute-start.12 = (bf16[256,1024]{1,0:T(8,128)(2,1)}, bf16[256,1024]{1,0:T(8,128)(2,1)}, u32[]{:S(2)}, u32[]{:S(2)}) collective-permute-start(bf16[256,1024]{1,0:T(8,128)(2,1)} %get-tuple-element.70), channel_id=1, source_target_pairs={{0,8},{24,16},{1,9},{25,17},{2,10},{26,18},{3,11},{27,19},{4,12},{... | collective-permute-start | bytes 1572872 | tf_op jit(solution)/shard_map/cond/branch_0_fun/ppermute | solution.py:37
  15.4 1.8 copy-start.12
  15.4 9.3 %copy-start.11 = (bf16[256,1024]{1,0:T(8,128)(2,1)S(1)}, bf16[256,1024]{1,0:T(8,128)(2,1)}, u32[]{:S(2)}) copy-start(bf16[256,1024]{1,0:T(8,128)(2,1)} %get-tuple-element.68) | copy-start | bytes 1572868 | tf_op jit(solution)/shard_map/cond
  17.1 29.9 %collective-permute-start.15 = (bf16[256,1024]{1,0:T(8,128)(2,1)S(1)}, bf16[256,1024]{1,0:T(8,128)(2,1)S(1)}, u32[]{:S(2)}, u32[]{:S(2)}) collective-permute-start(bf16[256,1024]{1,0:T(8,128)(2,1)S(1)} %copy-done.12), channel_id=1, source_target_pairs={{0,8},{24,16},{1,9},{25,17},{2,10},{26,18},{3,11},{27,19},{4,12},{... | collective-permute-start | bytes 1572872 | tf_op jit(solution)/shard_map/cond/branch_0_fun/ppermute | solution.py:37
  24.7 33.6 %collective-permute-start.18 = (bf16[256,1024]{1,0:T(8,128)(2,1)S(1)}, bf16[256,1024]{1,0:T(8,128)(2,1)S(1)}, u32[]{:S(2)}, u32[]{:S(2)}) collective-permute-start(bf16[256,1024]{1,0:T(8,128)(2,1)S(1)} %copy-done.11), channel_id=1, source_target_pairs={{0,8},{24,16},{1,9},{25,17},{2,10},{26,18},{3,11},{27,19},{4,12},{... | collective-permute-start | bytes 1572872 | tf_op jit(solution)/shard_map/cond/branch_0_fun/ppermute | solution.py:37
  30.5 29.6 %copy-start.9 = (bf16[256,1024]{1,0:T(8,128)(2,1)S(1)}, bf16[256,1024]{1,0:T(8,128)(2,1)}, u32[]{:S(2)}) copy-start(bf16[256,1024]{1,0:T(8,128)(2,1)} %get-tuple-element.27.refs_0_) | copy-start | bytes 1572868 | tf_op jit(solution)/shard_map/cond
  35.9 23.3 %collective-permute-start.2 = (bf16[256,1024]{1,0:T(8,128)(2,1)S(1)}, bf16[256,1024]{1,0:T(8,128)(2,1)S(1)}, u32[]{:S(2)}, u32[]{:S(2)}) collective-permute-start(bf16[256,1024]{1,0:T(8,128)(2,1)S(1)} %collective-permute-done.1.refs_2_), channel_id=1, source_target_pairs={{0,2},{2,0},{4,6},{6,4},{1,3},{3,1},{5,7},{7,5},{8,10},{10,8},{12,... | collective-permute-start | bytes 1572872 | tf_op jit(solution)/shard_map/cond/branch_0_fun/ppermute | solution.py:37
  37.3 32.2 %collective-permute-start.21 = (bf16[512,512]{1,0:T(8,128)(2,1)S(1)}, bf16[512,512]{1,0:T(8,128)(2,1)S(1)}, u32[]{:S(2)}, u32[]{:S(2)}) collective-permute-start(bf16[512,512]{1,0:T(8,128)(2,1)S(1)} %get-tuple-element.65), channel_id=1, source_target_pairs={{0,8},{8,0},{16,24},{24,16},{1,9},{9,1},{17,25},{25,17},{2,10},{10... | collective-permute-start | bytes 1572872 | tf_op jit(solution)/shard_map/cond/branch_0_fun/ppermute | solution.py:37
  39.9 40.9 %collective-permute-start.23 = (bf16[512,512]{1,0:T(8,128)(2,1)S(1)}, bf16[512,512]{1,0:T(8,128)(2,1)S(1)}, u32[]{:S(2)}, u32[]{:S(2)}) collective-permute-start(bf16[512,512]{1,0:T(8,128)(2,1)S(1)} %get-tuple-element.64), channel_id=1, source_target_pairs={{0,8},{8,0},{16,24},{24,16},{1,9},{9,1},{17,25},{25,17},{2,10},{10... | collective-permute-start | bytes 1572872 | tf_op jit(solution)/shard_map/cond/branch_0_fun/ppermute | solution.py:37
  47.0 44.9 %collective-permute-start.6 = (bf16[512,512]{1,0:T(8,128)(2,1)S(1)}, bf16[512,512]{1,0:T(8,128)(2,1)S(1)}, u32[]{:S(2)}, u32[]{:S(2)}) collective-permute-start(bf16[512,512]{1,0:T(8,128)(2,1)S(1)} %get-tuple-element.66), channel_id=1, source_target_pairs={{0,8},{8,0},{16,24},{24,16},{1,9},{9,1},{17,25},{25,17},{2,10},{10... | collective-permute-start | bytes 1572872 | tf_op jit(solution)/shard_map/cond/branch_0_fun/ppermute | solution.py:37
  58.3 36.3 %collective-permute-start.10 = (bf16[256,1024]{1,0:T(8,128)(2,1)S(1)}, bf16[256,1024]{1,0:T(8,128)(2,1)S(1)}, u32[]{:S(2)}, u32[]{:S(2)}) collective-permute-start(bf16[256,1024]{1,0:T(8,128)(2,1)S(1)} %add_convert_fusion.3), channel_id=1, source_target_pairs={{8,16},{16,8},{9,17},{17,9},{10,18},{18,10},{11,19},{19,11},{12,20... | collective-permute-start | bytes 1572872 | tf_op jit(solution)/shard_map/cond/branch_0_fun/ppermute | solution.py:37
  59.2 36.3 %collective-permute-start.13 = (bf16[256,1024]{1,0:T(8,128)(2,1)S(1)}, bf16[256,1024]{1,0:T(8,128)(2,1)S(1)}, u32[]{:S(2)}, u32[]{:S(2)}) collective-permute-start(bf16[256,1024]{1,0:T(8,128)(2,1)S(1)} %add_convert_fusion.2), channel_id=1, source_target_pairs={{8,16},{16,8},{9,17},{17,9},{10,18},{18,10},{11,19},{19,11},{12,20... | collective-permute-start | bytes 1572872 | tf_op jit(solution)/shard_map/cond/branch_0_fun/ppermute | solution.py:37
  69.5 61.2 %collective-permute-start.8 = (bf16[256,1024]{1,0:T(8,128)(2,1)S(1)}, bf16[256,1024]{1,0:T(8,128)(2,1)S(1)}, u32[]{:S(2)}, u32[]{:S(2)}) collective-permute-start(bf16[256,1024]{1,0:T(8,128)(2,1)S(1)} %get-tuple-element.72.refs_4_), channel_id=1, source_target_pairs={{0,1},{1,0},{2,3},{3,2},{4,5},{5,4},{6,7},{7,6},{8,9},{9,8},{10,11... | collective-permute-start | bytes 1572872 | tf_op jit(solution)/shard_map/cond/branch_0_fun/ppermute | solution.py:37
  80.7 51.3 %collective-permute-start.4 = (bf16[512,512]{1,0:T(8,128)(2,1)S(1)}, bf16[512,512]{1,0:T(8,128)(2,1)S(1)}, u32[]{:S(2)}, u32[]{:S(2)}) collective-permute-start(bf16[512,512]{1,0:T(8,128)(2,1)S(1)} %get-tuple-element.67), channel_id=1, source_target_pairs={{0,8},{8,0},{16,24},{24,16},{1,9},{9,1},{17,25},{25,17},{2,10},{10... | collective-permute-start | bytes 1572872 | tf_op jit(solution)/shard_map/cond/branch_0_fun/ppermute | solution.py:37
  92.0 11.7 %collective-permute-start.16 = (bf16[256,1024]{1,0:T(8,128)(2,1)S(1)}, bf16[256,1024]{1,0:T(8,128)(2,1)S(1)}, u32[]{:S(2)}, u32[]{:S(2)}) collective-permute-start(bf16[256,1024]{1,0:T(8,128)(2,1)S(1)} %add_convert_fusion.1), channel_id=1, source_target_pairs={{8,16},{16,8},{9,17},{17,9},{10,18},{18,10},{11,19},{19,11},{12,20... | collective-permute-start | bytes 1572872 | tf_op jit(solution)/shard_map/cond/branch_0_fun/ppermute | solution.py:37
  94.5 34.5 %collective-permute-start.19 = (bf16[256,1024]{1,0:T(8,128)(2,1)S(1)}, bf16[256,1024]{1,0:T(8,128)(2,1)S(1)}, u32[]{:S(2)}, u32[]{:S(2)}) collective-permute-start(bf16[256,1024]{1,0:T(8,128)(2,1)S(1)} %add_convert_fusion), channel_id=1, source_target_pairs={{8,16},{16,8},{9,17},{17,9},{10,18},{18,10},{11,19},{19,11},{12,20... | collective-permute-start | bytes 1572872 | tf_op jit(solution)/shard_map/cond/branch_0_fun/ppermute | solution.py:37
  95.5 60.1 %collective-permute-start.22 = (bf16[512,512]{1,0:T(8,128)(2,1)S(1)}, bf16[512,512]{1,0:T(8,128)(2,1)S(1)}, u32[]{:S(2)}, u32[]{:S(2)}) collective-permute-start(bf16[512,512]{1,0:T(8,128)(2,1)S(1)} %branch_0_fun.15.refs_0_), channel_id=1, source_target_pairs={{0,16},{8,24},{16,0},{24,8},{1,17},{9,25},{17,1},{25,9},{2,18},{10... | collective-permute-start | bytes 1572872 | tf_op jit(solution)/shard_map/cond/branch_0_fun/ppermute | solution.py:37
  103.7 60.8 %collective-permute-start.24 = (bf16[512,512]{1,0:T(8,128)(2,1)S(1)}, bf16[512,512]{1,0:T(8,128)(2,1)S(1)}, u32[]{:S(2)}, u32[]{:S(2)}) collective-permute-start(bf16[512,512]{1,0:T(8,128)(2,1)S(1)} %branch_0_fun.16.refs_1_), channel_id=1, source_target_pairs={{0,16},{8,24},{16,0},{24,8},{1,17},{9,25},{17,1},{25,9},{2,18},{10... | collective-permute-start | bytes 1572872 | tf_op jit(solution)/shard_map/cond/branch_0_fun/ppermute | solution.py:37
  129.0 46.8 %collective-permute-start.11 = (bf16[256,1024]{1,0:T(8,128)(2,1)S(1)}, bf16[256,1024]{1,0:T(8,128)(2,1)S(1)}, u32[]{:S(2)}, u32[]{:S(2)}) collective-permute-start(bf16[256,1024]{1,0:T(8,128)(2,1)S(1)} %multiply_convert_fusion.3.refs_4_), channel_id=1, source_target_pairs={{8,0},{16,24},{9,1},{17,25},{10,2},{18,26},{11,3},{19,27},{12,4},{... | collective-permute-start | bytes 1572872 | tf_op jit(solution)/shard_map/cond/branch_0_fun/ppermute | solution.py:37
  130.7 60.4 %collective-permute-start.14 = (bf16[256,1024]{1,0:T(8,128)(2,1)S(1)}, bf16[256,1024]{1,0:T(8,128)(2,1)S(1)}, u32[]{:S(2)}, u32[]{:S(2)}) collective-permute-start(bf16[256,1024]{1,0:T(8,128)(2,1)S(1)} %multiply_convert_fusion.2.refs_6_), channel_id=1, source_target_pairs={{8,0},{16,24},{9,1},{17,25},{10,2},{18,26},{11,3},{19,27},{12,4},{... | collective-permute-start | bytes 1572872 | tf_op jit(solution)/shard_map/cond/branch_0_fun/ppermute | solution.py:37
  132.0 88.7 %collective-permute-start.17 = (bf16[256,1024]{1,0:T(8,128)(2,1)S(1)}, bf16[256,1024]{1,0:T(8,128)(2,1)S(1)}, u32[]{:S(2)}, u32[]{:S(2)}) collective-permute-start(bf16[256,1024]{1,0:T(8,128)(2,1)S(1)} %multiply_convert_fusion.1.refs_8_), channel_id=1, source_target_pairs={{8,0},{16,24},{9,1},{17,25},{10,2},{18,26},{11,3},{19,27},{12,4},{... | collective-permute-start | bytes 1572872 | tf_op jit(solution)/shard_map/cond/branch_0_fun/ppermute | solution.py:37
  155.6 75.3 %collective-permute-start.20 = (bf16[256,1024]{1,0:T(8,128)(2,1)S(1)}, bf16[256,1024]{1,0:T(8,128)(2,1)S(1)}, u32[]{:S(2)}, u32[]{:S(2)}) collective-permute-start(bf16[256,1024]{1,0:T(8,128)(2,1)S(1)} %multiply_convert_fusion.refs_10_), channel_id=1, source_target_pairs={{8,0},{16,24},{9,1},{17,25},{10,2},{18,26},{11,3},{19,27},{12,4},{... | collective-permute-start | bytes 1572872 | tf_op jit(solution)/shard_map/cond/branch_0_fun/ppermute | solution.py:37
  164.5 76.7 %collective-permute-start.7 = (bf16[512,512]{1,0:T(8,128)(2,1)S(1)}, bf16[512,512]{1,0:T(8,128)(2,1)S(1)}, u32[]{:S(2)}, u32[]{:S(2)}) collective-permute-start(bf16[512,512]{1,0:T(8,128)(2,1)S(1)} %branch_0_fun.12.refs_1_), channel_id=1, source_target_pairs={{0,16},{8,24},{16,0},{24,8},{1,17},{9,25},{17,1},{25,9},{2,18},{10... | collective-permute-start | bytes 1572872 | tf_op jit(solution)/shard_map/cond/branch_0_fun/ppermute | solution.py:37
  175.8 65.4 %collective-permute-start.5 = (bf16[512,512]{1,0:T(8,128)(2,1)S(1)}, bf16[512,512]{1,0:T(8,128)(2,1)S(1)}, u32[]{:S(2)}, u32[]{:S(2)}) collective-permute-start(bf16[512,512]{1,0:T(8,128)(2,1)S(1)} %branch_0_fun.11.refs_0_), channel_id=1, source_target_pairs={{0,16},{8,24},{16,0},{24,8},{1,17},{9,25},{17,1},{25,9},{2,18},{10... | collective-permute-start | bytes 1572872 | tf_op jit(solution)/shard_map/cond/branch_0_fun/ppermute | solution.py:37
  251.6 1.3 copy-start.3
  251.6 2.0 copy-start.7
